TPU v7x, 128 devices: a whole 4x4x4 slice. The times are simulated.
128 devices in a mesh: dp: 64 (over z, x_lo, y, core), tensor: 2 (over x_hi).
Axes of the slice: x: 4 (x_hi: 2, x_lo: 2; x = x_hi * 2 + x_lo), y: 4, z: 4, core: 2. Of those that a mesh axis runs over, the one named last changes fastest.
Arguments:
- hidden_in: bfloat16 [32768, 1024], P('dp'), may hold values from -16 to 16
- segment_ids: int32 [32768], P('dp'), may hold values from 0 to 79, never falling along the last dimension, each value on 1 to 2048 neighbouring positions
- ln_one_gain: float32 [1024], replicated, may hold values from 0.25 to 1.75
- ln_one_bias: float32 [1024], replicated, may hold values from -1.75 to 1.75
- w_query: bfloat16 [1024, 1024], P(None, 'tensor'), may hold values from -0.1875 to 0.1875
- w_key: bfloat16 [1024, 1024], P(None, 'tensor'), may hold values from -0.1875 to 0.1875
- w_value: bfloat16 [1024, 1024], P(None, 'tensor'), may hold values from -0.1875 to 0.1875
- b_query: float32 [1024], P('tensor'), may hold values from -3 to 3
- b_value: float32 [1024], P('tensor'), may hold values from -3 to 3
- w_out: bfloat16 [1024, 1024], P('tensor'), may hold values from -0.75 to 0.75
- b_out: float32 [1024], replicated, may hold values from -1.75 to 1.75
- ln_two_gain: float32 [1024], replicated, may hold values from 0.25 to 1.75
- ln_two_bias: float32 [1024], replicated, may hold values from -1.75 to 1.75
- w_fc: bfloat16 [1024, 4096], P(None, 'tensor'), may hold values from -0.1875 to 0.1875
- b_fc: float32 [4096], P('tensor'), may hold values from -3 to 3
- w_proj: bfloat16 [4096, 1024], P('tensor'), may hold values from -0.09375 to 0.09375
- b_proj: float32 [1024], replicated, may hold values from -1.75 to 1.75
- cotangent: float32 [32768, 1024], P('dp'), may hold values from -16 to 16
Outputs:
- block_out: float32 [32768, 1024], P('dp')
- input_grad: float32 [32768, 1024], P('dp')
- grad_ln_one_gain: float32 [1024], replicated
- grad_ln_one_bias: float32 [1024], replicated
- grad_query: float32 [1024, 1024], P('dp', 'tensor')
- grad_key: float32 [1024, 1024], P('dp', 'tensor')
- grad_value: float32 [1024, 1024], P('dp', 'tensor')
- grad_b_query: float32 [1024], P('tensor')
- grad_b_value: float32 [1024], P('tensor')
- grad_w_out: float32 [1024, 1024], P('tensor', 'dp')
- grad_b_out: float32 [1024], replicated
- grad_ln_two_gain: float32 [1024], replicated
- grad_ln_two_bias: float32 [1024], replicated
- grad_fc: float32 [1024, 4096], P('dp', 'tensor')
- grad_b_fc: float32 [4096], P('tensor')
- grad_proj: float32 [4096, 1024], P('tensor', 'dp')
- grad_b_proj: float32 [1024], replicated
All inputs are finite; a program needn't handle non-finite values.
Results may differ from a plain program's by a relative error of at most 0.012.
Values sent between devices are 32-bit elements; how exact they have to be, the bound alone decides.
A program may use at most 256 MiB of HBM per device.

v0:
```python
import jax
import jax.numpy as jnp
from jax import lax
from jax.sharding import PartitionSpec as P

HEAD_DIM = 64
SEQ = 512


EPS = 1e-05
GELU_C = 0.7978845608028654
CUBIC = 0.044715


def from_everyone(value, axis):
    devices = lax.axis_size(axis)
    return lax.all_to_all(
        jnp.broadcast_to(value[None], (devices, *value.shape)), axis, 0, 0, tiled=True
    )


def taken_together(value, axis):
    return from_everyone(value, axis).sum(axis=0)


def cut_along(value, dim, devices):
    shape = value.shape
    blocks = value.reshape(*shape[:dim], devices, shape[dim] // devices, *shape[dim + 1 :])
    return jnp.moveaxis(blocks, dim, 0)


def sum_together(arrays, axis, dims):
    devices = lax.axis_size(axis)
    blocks = [cut_along(a, dim, devices) for a, dim in zip(arrays, dims)]
    lines = jnp.concatenate([b.reshape(devices, -1) for b in blocks], axis=1)
    rows = max(16, -(-lines.shape[1] // 1024) * 8)
    lines = jnp.pad(lines, ((0, 0), (0, rows * 128 - lines.shape[1]))).reshape(-1, 128)
    line, at, gathered = (lax.psum_scatter(lines, axis, tiled=True).reshape(-1), 0, [])
    for b in blocks:
        part = b[0]
        gathered.append(line[at : at + part.size].reshape(part.shape))
        at += part.size
    return tuple(gathered)


def packed_total(arrays, axis):
    line, at, gathered = (jnp.concatenate([a.reshape(-1) for a in arrays]), 0, [])
    so_far = taken_together(line, axis)
    for a in arrays:
        gathered.append(so_far[at : at + a.size].reshape(a.shape))
        at += a.size
    return tuple(gathered)


def layer_norm(values, gain, shift):
    centre = values - jnp.mean(values, axis=-1, keepdims=True)
    inverse = lax.rsqrt(jnp.mean(centre * centre, axis=-1, keepdims=True) + EPS)
    normed = centre * inverse
    return (normed * gain + shift, normed, inverse)


def norm_backward(grad_out, normed, inverse, gain):
    scaled = grad_out * gain
    grad_rows = inverse * (
        scaled
        - jnp.mean(scaled, axis=-1, keepdims=True)
        - normed * jnp.mean(scaled * normed, axis=-1, keepdims=True)
    )
    return (grad_rows, jnp.sum(grad_out * normed, axis=0), jnp.sum(grad_out, axis=0))


def gelu_parts(inner):
    tangent = jnp.tanh(GELU_C * (inner + CUBIC * inner * inner * inner))
    value = 0.5 * inner * (1.0 + tangent)
    slope = 0.5 * (1.0 + tangent) + 0.5 * inner * (1.0 - tangent * tangent) * GELU_C * (
        1.0 + 3.0 * CUBIC * inner * inner
    )
    return (value, slope)


def fdot(left, right):
    return jnp.dot(left, right, preferred_element_type=jnp.float32)


def contract_rows(left, right):
    return jnp.einsum("ta,tb->ab", left, right, preferred_element_type=jnp.float32)


def contract_cols(left, right):
    return jnp.einsum("ta,ba->tb", left, right, preferred_element_type=jnp.float32)


def allowed_mask(segments):
    rows = lax.broadcasted_iota(jnp.int32, (SEQ, SEQ), 0)
    cols = lax.broadcasted_iota(jnp.int32, (SEQ, SEQ), 1)
    same = segments[:, :, None] == segments[:, None, :]
    return (same & (cols <= rows)[None])[:, None]


def masked_scores(query, keys, allowed):
    scale = 1.0 / HEAD_DIM**0.5
    scores = jnp.einsum("bqhd,bkhd->bhqk", query, keys, preferred_element_type=jnp.float32) * scale
    return jnp.where(allowed, scores, -1e30)


def attend_forward(query, keys, values, allowed):
    masked = masked_scores(query, keys, allowed)
    top = jnp.max(masked, axis=-1, keepdims=True)
    log_total = top + jnp.log(jnp.sum(jnp.exp(masked - top), axis=-1, keepdims=True))
    probs = jnp.exp(masked - log_total).astype(jnp.bfloat16)
    attended = jnp.einsum("bhqk,bkhd->bqhd", probs, values, preferred_element_type=jnp.float32)
    return (attended.astype(jnp.bfloat16), log_total)


def attend_backward(query, keys, values, allowed, log_total, grad_attended):
    scale = 1.0 / HEAD_DIM**0.5
    probs_f = jnp.exp(masked_scores(query, keys, allowed) - log_total)
    probs = probs_f.astype(jnp.bfloat16)
    grad_probs = jnp.einsum(
        "bqhd,bkhd->bhqk", grad_attended, values, preferred_element_type=jnp.float32
    )
    delta = jnp.sum(probs_f * grad_probs, axis=-1, keepdims=True)
    grad_scores = (probs_f * (grad_probs - delta) * scale).astype(jnp.bfloat16)
    grad_q = jnp.einsum("bhqk,bkhd->bqhd", grad_scores, keys, preferred_element_type=jnp.float32)
    grad_k = jnp.einsum("bhqk,bqhd->bkhd", grad_scores, query, preferred_element_type=jnp.float32)
    grad_v = jnp.einsum("bhqk,bqhd->bkhd", probs, grad_attended, preferred_element_type=jnp.float32)
    return (grad_q, grad_k, grad_v)


def on_device(
    hidden_in,
    segment_ids,
    ln_one_gain,
    ln_one_bias,
    w_query,
    w_key,
    w_value,
    b_query,
    b_value,
    w_out,
    b_out,
    ln_two_gain,
    ln_two_bias,
    w_fc,
    b_fc,
    w_proj,
    b_proj,
    cotangent,
):
    tok_rows = hidden_in.shape[0]
    seq_count = tok_rows // SEQ
    local_width = w_query.shape[1]
    local_heads = local_width // HEAD_DIM

    def split_heads(flat):
        return flat.reshape(seq_count, SEQ, local_heads, HEAD_DIM)

    inputs = hidden_in.astype(jnp.float32)
    first_f, normed_one, inverse_one = layer_norm(inputs, ln_one_gain, ln_one_bias)
    first_in = first_f.astype(jnp.bfloat16)
    query = split_heads((fdot(first_in, w_query) + b_query).astype(jnp.bfloat16))
    keys = split_heads(fdot(first_in, w_key).astype(jnp.bfloat16))
    values = split_heads((fdot(first_in, w_value) + b_value).astype(jnp.bfloat16))
    allowed = allowed_mask(segment_ids.reshape(seq_count, SEQ))
    attended, log_total = attend_forward(query, keys, values, allowed)
    attended_flat = attended.reshape(tok_rows, local_width)
    attn_total = taken_together(fdot(attended_flat, w_out), "tensor")
    middle = inputs + attn_total + b_out
    second_f, normed_two, inverse_two = layer_norm(middle, ln_two_gain, ln_two_bias)
    second_in = second_f.astype(jnp.bfloat16)
    inner = fdot(second_in, w_fc) + b_fc
    activated_f, slope = gelu_parts(inner)
    activated = activated_f.astype(jnp.bfloat16)
    mlp_total = taken_together(fdot(activated, w_proj), "tensor")
    block_out = middle + mlp_total + b_proj
    top_grad = cotangent.astype(jnp.bfloat16)
    grad_b_proj = jnp.sum(cotangent, axis=0)
    grad_proj = contract_rows(activated, top_grad)
    grad_inner = contract_cols(top_grad, w_proj) * slope
    grad_b_fc = jnp.sum(grad_inner, axis=0)
    grad_inner_b = grad_inner.astype(jnp.bfloat16)
    grad_fc = contract_rows(second_in, grad_inner_b)
    grad_second = taken_together(contract_cols(grad_inner_b, w_fc), "tensor")
    rows_two, grad_ln_two_gain, grad_ln_two_bias = norm_backward(
        grad_second, normed_two, inverse_two, ln_two_gain
    )
    grad_middle = cotangent + rows_two
    grad_b_out = jnp.sum(grad_middle, axis=0)
    middle_b = grad_middle.astype(jnp.bfloat16)
    grad_w_out = contract_rows(attended_flat, middle_b)
    grad_attended = contract_cols(middle_b, w_out).astype(jnp.bfloat16)
    grad_q, grad_k, grad_v = attend_backward(
        query, keys, values, allowed, log_total, split_heads(grad_attended)
    )
    grad_q = grad_q.reshape(tok_rows, local_width)
    grad_k = grad_k.reshape(tok_rows, local_width)
    grad_v = grad_v.reshape(tok_rows, local_width)
    grad_b_query = jnp.sum(grad_q, axis=0)
    grad_b_value = jnp.sum(grad_v, axis=0)
    grad_q_b = grad_q.astype(jnp.bfloat16)
    grad_k_b = grad_k.astype(jnp.bfloat16)
    grad_v_b = grad_v.astype(jnp.bfloat16)
    grad_query = contract_rows(first_in, grad_q_b)
    grad_key = contract_rows(first_in, grad_k_b)
    grad_value = contract_rows(first_in, grad_v_b)
    first_terms = (
        contract_cols(grad_q_b, w_query)
        + contract_cols(grad_k_b, w_key)
        + contract_cols(grad_v_b, w_value)
    )
    grad_first = taken_together(first_terms, "tensor")
    rows_one, grad_ln_one_gain, grad_ln_one_bias = norm_backward(
        grad_first, normed_one, inverse_one, ln_one_gain
    )
    input_grad = grad_middle + rows_one
    query_share, key_share, value_share, out_share, fc_share, proj_share = sum_together(
        (grad_query, grad_key, grad_value, grad_w_out, grad_fc, grad_proj), "dp", (0, 0, 0, 1, 0, 1)
    )
    small = packed_total(
        (
            grad_ln_one_gain,
            grad_ln_one_bias,
            grad_b_query,
            grad_b_value,
            grad_b_out,
            grad_ln_two_gain,
            grad_ln_two_bias,
            grad_b_fc,
            grad_b_proj,
        ),
        "dp",
    )
    return (
        block_out,
        input_grad,
        small[0],
        small[1],
        query_share,
        key_share,
        value_share,
        small[2],
        small[3],
        out_share,
        small[4],
        small[5],
        small[6],
        fc_share,
        small[7],
        proj_share,
        small[8],
    )


def solution(mesh):
    in_specs = (
        P("dp", None),
        P("dp"),
        P(),
        P(),
        P(None, "tensor"),
        P(None, "tensor"),
        P(None, "tensor"),
        P("tensor"),
        P("tensor"),
        P("tensor", None),
        P(),
        P(),
        P(),
        P(None, "tensor"),
        P("tensor"),
        P("tensor", None),
        P(),
        P("dp", None),
    )
    out_specs = (
        P("dp", None),
        P("dp", None),
        P(),
        P(),
        P("dp", "tensor"),
        P("dp", "tensor"),
        P("dp", "tensor"),
        P("tensor"),
        P("tensor"),
        P("tensor", "dp"),
        P(),
        P(),
        P(),
        P("dp", "tensor"),
        P("tensor"),
        P("tensor", "dp"),
        P(),
    )
    return jax.shard_map(
        on_device, mesh=mesh, in_specs=in_specs, out_specs=out_specs, check_vma=False
    )
```

profile of v0, /device:TPU:0, one launch (start us, length us, event | category | flops | bytes accessed | tf_op | source)
XLA Modules:
  0.0 761.9 jit_solution(15306128592433364946)
XLA Ops:
  24.3 53.3 %all_to_all.26 = f32[2,512,1024]{2,1,0:T(8,128)} all-to-all(f32[2,512,1024]{2,1,0:T(8,128)S(1)} %broadcast_in_dim.28), channel_id=1, replica_groups=mesh['dp'=64,'tensor'=2] {'tensor'}, dimensions={0} | all-to-all | bytes 8388608 | tf_op jit(solution)/shard_map/all_to_all | solution.py:17
  87.6 5.4 fusion.103
  97.9 5.7 all-to-all-start.2
  103.6 7.6 fusion.80
  111.1 40.5 %all-to-all-done.2 = f32[2,512,1024]{2,1,0:T(8,128)} async-done(((f32[2,512,1024]{2,1,0:T(8,128)}), f32[2,512,1024]{2,1,0:T(8,128)}, u32[]{:S(2)}, u32[]{:S(2)}) %all-to-all-start.2) | async-done | bytes 4194336 | tf_op jit(solution)/shard_map/all_to_all | solution.py:17
  155.7 5.6 all-to-all-start.1
  161.4 7.4 fusion.58
  168.7 9.8 %reshape_reshape.15 = f32[64,32768]{1,0:T(8,128)} reshape(f32[1024,2048]{1,0:T(8,128)} %fusion.58) | data formatting | bytes 16777216 | tf_op jit(solution)/shard_map/reshape;reshape | solution.py:35
  178.5 12.2 %copy.108 = f32[64,32768]{0,1:T(8,128)} copy(f32[64,32768]{1,0:T(8,128)} %reshape_reshape.15) | data formatting | bytes 16777216 | tf_op jit(solution)/shard_map/reshape;reshape | solution.py:35
  190.7 8.6 %fusion.64 = f32[2048,1024]{0,1:T(8,128)} fusion(f32[512,1024]{1,0:T(8,128)} %param.35, f32[512,2048]{1,0:T(8,128)} %copy-done.41, f32[2048]{0:T(1024)S(1)} %copy-done.35), kind=kOutput, calls=%fused_computation.76 | convolution fusion | flops 2158493696 | bytes 14688256 | tf_op jit(solution)/shard_map/ta,tb->ab/dot_general | solution.py:86
  199.3 15.5 %copy.104 = f32[2048,64,16]{1,2,0:T(8,128)} copy(f32[2048,64,16]{0,2,1:T(8,128)} %bitcast.70) | data formatting | bytes 16777216 | tf_op jit(solution)/shard_map/reshape | solution.py:28
  230.6 4.5 fusion.105
  235.1 13.4 %fusion.96 = (f32[8,64]{1,0:T(8,128)S(1)}, bf16[1,512,8,64]{1,3,2,0:T(8,128)(2,1)S(1)}) fusion(bf16[512,8,64]{0,2,1:T(8,128)(2,1)S(1)} %bitcast.79, f32[8,512,512]{1,2,0:T(8,128)} %fusion.105, f32[8,512,512]{1,2,0:T(8,128)} %copy-done.2, f32[8,512]{1,0:T(8,128)S(1)} %log_add_fusion, pred[512,512]{0,1:T(8,128)(4,1)S(1)} %fusion.62), kind=kOutput, calls=%fused_computation.119 | convolution fusion | flops 292032512 | bytes 18106368 | tf_op jit(solution)/shard_map/bhqk,bkhd->bqhd/dot_general | solution.py:124
  248.5 14.4 %fusion.54 = bf16[8,64,512]{2,1,0:T(8,128)(2,1)} fusion(bf16[512,8,64]{0,2,1:T(8,128)(2,1)S(1)} %bitcast.77, f32[8,512,512]{1,2,0:T(8,128)} %fusion.105, f32[8,512,512]{1,2,0:T(8,128)} %copy-done.2, f32[8,512]{1,0:T(8,128)S(1)} %log_add_fusion, pred[512,512]{0,1:T(8,128)(4,1)S(1)} %fusion.62), kind=kOutput, calls=%fused_computation.64 | convolution fusion | flops 291770880 | bytes 18104320 | tf_op jit(solution)/shard_map/bhqk,bqhd->bkhd/dot_general | solution.py:125
  262.9 6.4 fusion.95
  303.7 4.6 constant_dynamic-update-slice_fusion.5
  314.4 13.4 %constant_dynamic-update-slice_fusion.2 = f32[64,98304]{0,1:T(8,128)} fusion(f32[64,98304]{0,1:T(8,128)} %constant_dynamic-update-slice_fusion.3, f32[64,32768]{0,1:T(8,128)} %copy.108), kind=kLoop, calls=%fused_computation.81 | loop fusion | bytes 33554432
  330.2 6.0 constant_dynamic-update-slice_fusion.1
  336.2 36.4 %copy.109 = f32[64,98304]{1,0:T(8,128)} copy(f32[64,98304]{0,1:T(8,128)} %constant_dynamic-update-slice_fusion.1) | data formatting | bytes 50331648 | tf_op jit(solution)/shard_map/concatenate | solution.py:35
  372.6 19.1 %reshape.288 = f32[49152,128]{1,0:T(8,128)} reshape(f32[64,98304]{1,0:T(8,128)} %copy.109) | data formatting | bytes 50331648 | tf_op jit(solution)/shard_map/reshape | solution.py:37
  398.4 5.7 all-to-all-start.3
  404.2 68.4 %all-to-all-done.3 = f32[2,512,1024]{2,1,0:T(8,128)} async-done(((f32[2,512,1024]{2,1,0:T(8,128)}), f32[2,512,1024]{2,1,0:T(8,128)}, u32[]{:S(2)}, u32[]{:S(2)}) %all-to-all-start.3) | async-done | bytes 4194336 | tf_op jit(solution)/shard_map/all_to_all | solution.py:17
  479.8 58.2 %all_to_all.27 = f32[64,1,9216]{2,1,0:T(1,128)S(1)} all-to-all(f32[64,1,9216]{2,1,0:T(1,128)S(1)} %broadcast_in_dim.32), channel_id=1, replica_groups=mesh['dp'=64,'tensor'=2] {'dp'}, dimensions={0} | all-to-all | bytes 4718592 | tf_op jit(solution)/shard_map/all_to_all | solution.py:17
  541.2 207.2 %reduce-scatter.2.cloned.1.call-done = f32[768,128]{1,0:T(8,128)} async-done(((f32[49152,128]{1,0:T(8,128)}), f32[768,128]{1,0:T(8,128)}) %reduce-scatter.2.cloned.1.call-update) | async-done | bytes 393232 | tf_op jit(solution)/shard_map/reduce_scatter | solution.py:38
  (175 shorter events, 118.1 us)
Async XLA Ops:
  7.2 15.8 %copy-start = (bf16[512,1024]{1,0:T(8,128)(2,1)S(1)}, bf16[512,1024]{1,0:T(8,128)(2,1)}, u32[]{:S(2)}) copy-start(bf16[512,1024]{1,0:T(8,128)(2,1)} %param.27) | copy-start | bytes 3145732
  7.2 6.8 copy-start.3
  7.2 6.8 copy-start.37
  7.2 6.8 copy-start.28
  7.2 6.8 copy-start.12
  7.3 6.8 copy-start.38
  87.6 5.4 copy-start.41
  97.9 53.7 %all-to-all-start.2 = ((f32[2,512,1024]{2,1,0:T(8,128)}), f32[2,512,1024]{2,1,0:T(8,128)}, u32[]{:S(2)}, u32[]{:S(2)}) async-start(f32[2,512,1024]{2,1,0:T(8,128)} %broadcast_in_dim.30), calls=%async_computation.2 | async-start | bytes 8388608 | tf_op jit(solution)/shard_map/all_to_all | solution.py:17
  155.7 64.2 %all-to-all-start.1 = ((f32[2,512,1024]{2,1,0:T(8,128)}), f32[2,512,1024]{2,1,0:T(8,128)}, u32[]{:S(2)}, u32[]{:S(2)}) async-start(f32[2,512,1024]{2,1,0:T(8,128)} %broadcast_in_dim.29), calls=%async_computation.1 | async-start | bytes 8388608 | tf_op jit(solution)/shard_map/all_to_all | solution.py:17
  161.3 587.1 %reduce-scatter.2.cloned.1.call-start = ((), (), s32[]{:S(2)}) async-start(), calls=%async_computation.6 | async-start | bytes 25559040 | tf_op jit(solution)/shard_map/reduce_scatter | solution.py:38
  224.0 6.6 copy-start.22
  230.6 4.5 copy-start.20
  235.1 13.4 %copy-start.18 = (bf16[512,512]{0,1:T(8,128)(2,1)S(1)}, bf16[512,512]{0,1:T(8,128)(2,1)}, u32[]{:S(2)}) copy-start(bf16[512,512]{0,1:T(8,128)(2,1)} %copy-done.17) | copy-start | bytes 1572868
  248.5 20.9 %copy-start.23 = (bf16[1,512,8,64]{1,3,2,0:T(8,128)(2,1)}, bf16[1,512,8,64]{1,3,2,0:T(8,128)(2,1)S(1)}, u32[]{:S(2)}) copy-start(bf16[1,512,8,64]{1,3,2,0:T(8,128)(2,1)S(1)} %get-tuple-element.106) | copy-start | bytes 1572868
  262.9 6.4 copy-start.4
  276.2 4.4 copy-start.25
  303.7 4.6 copy-start.8
  312.0 15.8 %slice-start = ((s8[16777216]{0:T(1024)(128)(4,1)}), s8[4194304]{0:T(1024)(128)(4,1)S(1)}, s32[]{:S(2)}) async-start(s8[16777216]{0:T(1024)(128)(4,1)} %bitcast.66), calls=%async_computation.7 | async-start | bytes 8388608
  314.4 13.4 %slice-start.1 = ((s8[16777216]{0:T(1024)(128)(4,1)}), s8[4194304]{0:T(1024)(128)(4,1)S(1)}, s32[]{:S(2)}) async-start(s8[16777216]{0:T(1024)(128)(4,1)} %bitcast.66), calls=%async_computation.8 | async-start | bytes 8388608
  314.4 14.6 %slice-start.2 = ((s8[16777216]{0:T(1024)(128)(4,1)}), s8[4194304]{0:T(1024)(128)(4,1)S(1)}, s32[]{:S(2)}) async-start(s8[16777216]{0:T(1024)(128)(4,1)} %bitcast.66), calls=%async_computation.9 | async-start | bytes 8388608
  314.4 15.8 %slice-start.3 = ((s8[16777216]{0:T(1024)(128)(4,1)}), s8[4194304]{0:T(1024)(128)(4,1)S(1)}, s32[]{:S(2)}) async-start(s8[16777216]{0:T(1024)(128)(4,1)} %bitcast.66), calls=%async_computation.10 | async-start | bytes 8388608
  398.4 74.2 %all-to-all-start.3 = ((f32[2,512,1024]{2,1,0:T(8,128)}), f32[2,512,1024]{2,1,0:T(8,128)}, u32[]{:S(2)}, u32[]{:S(2)}) async-start(f32[2,512,1024]{2,1,0:T(8,128)} %broadcast_in_dim.31), calls=%async_computation.3 | async-start | bytes 8388608 | tf_op jit(solution)/shard_map/all_to_all | solution.py:17
  404.2 72.3 %copy-start.6 = (f32[512,1024]{1,0:T(8,128)S(1)}, f32[512,1024]{1,0:T(8,128)}, u32[]{:S(2)}) copy-start(f32[512,1024]{1,0:T(8,128)} %copy-done.5) | copy-start | bytes 6291460
  479.8 275.0 %copy-start.1 = (bf16[512,1024]{1,0:T(8,128)(2,1)S(1)}, bf16[512,1024]{1,0:T(8,128)(2,1)}, u32[]{:S(2)}) copy-start(bf16[512,1024]{1,0:T(8,128)(2,1)} %param.27) | copy-start | bytes 3145732
  (26 other events, 61.1 us)
Sparse Core Ops, SparseCore 0:
  391.9 356.4 reduce-scatter.1
where the time goes:
time: 771 us; the launch traced here: 762 us
  waiting for transfers between devices  316 us (41%)
  local copies, waits for them, and re-layouts  175 us (23%)
  blocking collectives  111 us (14%)
  matrix products  94.8 us (12%)
  other arithmetic  32.4 us (4%)
  starting transfers between devices  17 us (2%)
  between operations  14.9 us (2%)
    reduce_scatter x1, waiting for transfers between devices, sum_together(): lax.psum_scatter(lines, axis, tiled=True).reshape(-1)  207 us
    all_to_all x2, blocking collectives, from_everyone(): lax.all_to_all(jnp.broadcast_to(value[None], (devices, *value.shape)), ax...  111 us
    all_to_all x3, waiting for transfers between devices, from_everyone(): lax.all_to_all(jnp.broadcast_to(value[None], (devices, *value.shape)), ax...  109 us
    concatenate x2, local copies, waits for them, and re-layouts, sum_together(): lines = jnp.concatenate([b.reshape(devices, -1) for b in blocks], axis=1)  42.4 us
    unnamed x107, local copies, waits for them, and re-layouts  39.2 us
    another operation x8, local copies, waits for them, and re-layouts, sum_together(): lines = jnp.concatenate([b.reshape(devices, -1) for b in blocks], axis=1)  35.4 us
    dot_general x6, matrix products, contract_rows(): jnp.einsum('ta,tb->ab', left, right, preferred_element_type=jnp.float32)  26.2 us
    reshape x1, local copies, waits for them, and re-layouts, sum_together(): jnp.pad(lines, ((0, 0), (0, rows * 128 - lines.shape[1]))).reshape(-1, 128)  19.1 us
  transfers between devices with their start and end apart: 4, of which 3 were waited for; matrix products, arithmetic and copies ran while one was open for 10% of the time, Pallas kernels for 0%

commit v1 on v0

--- a/solution.py
+++ b/solution.py
@@ -1,6 +1,10 @@
+import functools
+
 import jax
 import jax.numpy as jnp
 from jax import lax
+from jax.experimental import pallas as pl
+from jax.experimental.pallas import tpu as pltpu
 from jax.sharding import PartitionSpec as P
 
 HEAD_DIM = 64
@@ -11,45 +15,300 @@
 GELU_C = 0.7978845608028654
 CUBIC = 0.044715
 
-
-def from_everyone(value, axis):
-    devices = lax.axis_size(axis)
-    return lax.all_to_all(
-        jnp.broadcast_to(value[None], (devices, *value.shape)), axis, 0, 0, tiled=True
-    )
-
-
-def taken_together(value, axis):
-    return from_everyone(value, axis).sum(axis=0)
-
-
-def cut_along(value, dim, devices):
-    shape = value.shape
-    blocks = value.reshape(*shape[:dim], devices, shape[dim] // devices, *shape[dim + 1 :])
-    return jnp.moveaxis(blocks, dim, 0)
-
-
-def sum_together(arrays, axis, dims):
-    devices = lax.axis_size(axis)
-    blocks = [cut_along(a, dim, devices) for a, dim in zip(arrays, dims)]
-    lines = jnp.concatenate([b.reshape(devices, -1) for b in blocks], axis=1)
-    rows = max(16, -(-lines.shape[1] // 1024) * 8)
-    lines = jnp.pad(lines, ((0, 0), (0, rows * 128 - lines.shape[1]))).reshape(-1, 128)
-    line, at, gathered = (lax.psum_scatter(lines, axis, tiled=True).reshape(-1), 0, [])
-    for b in blocks:
-        part = b[0]
-        gathered.append(line[at : at + part.size].reshape(part.shape))
-        at += part.size
-    return tuple(gathered)
-
-
-def packed_total(arrays, axis):
-    line, at, gathered = (jnp.concatenate([a.reshape(-1) for a in arrays]), 0, [])
-    so_far = taken_together(line, axis)
-    for a in arrays:
-        gathered.append(so_far[at : at + a.size].reshape(a.shape))
-        at += a.size
-    return tuple(gathered)
+MESH = pl.DeviceIdType.MESH
+IN_PLACE = pl.BlockSpec(memory_space=pl.ANY)
+IN_VMEM = pl.BlockSpec(memory_space=pltpu.VMEM)
+
+
+def place():
+    dp = lax.axis_index("dp")
+    return dict(z=dp // 16, x=(dp // 8) % 2, y=(dp // 2) % 4, c=dp % 2, t=lax.axis_index("tensor"))
+
+
+def device(p, **change):
+    q = dict(p, **change)
+    return {"dp": q["z"] * 16 + q["x"] * 8 + q["y"] * 2 + q["c"], "tensor": q["t"]}
+
+
+def neighbours(p):
+    near = {"partner": device(p, t=1 - p["t"]), "core": device(p, c=1 - p["c"]), "x": device(p, x=1 - p["x"])}
+    for axis in "yz":
+        for step, name in ((1, "up"), (2, "far"), (3, "down")):
+            near[f"{axis}_{name}"] = device(p, **{axis: (p[axis] + step) % 4})
+    return near
+
+
+def greet(peers):
+    barrier = pltpu.get_barrier_semaphore()
+    for peer in peers:
+        pl.semaphore_signal(barrier, inc=1, device_id=peer, device_id_type=MESH)
+    pl.semaphore_wait(barrier, len(peers))
+
+
+def remote(src, dst, sems, i, to):
+    return pltpu.make_async_remote_copy(
+        src_ref=src,
+        dst_ref=dst,
+        send_sem=sems.at[0, i],
+        recv_sem=sems.at[1, i],
+        device_id=to,
+        device_id_type=MESH,
+    )
+
+
+CORE, VIA, DIRECT, VIA2, DIRECT2, LAST, COPIES = 0, 8, 10, 14, 16, 20, 21
+ORDER = (2, 1, 3, 0)
+
+
+def scatter_scratch(width):
+    return [
+        pltpu.VMEM((4, 2, 4, 16, width), jnp.float32),
+        pltpu.VMEM((4, 2, 4, 16, width), jnp.float32),
+        pltpu.VMEM((2, 4, 16, width), jnp.float32),
+        pltpu.VMEM((2, 2, 4, 16, width), jnp.float32),
+        pltpu.VMEM((2, 16, width), jnp.float32),
+        pltpu.VMEM((2, 2, 16, width), jnp.float32),
+        pltpu.VMEM((16, width), jnp.float32),
+        pltpu.SemaphoreType.DMA((2, COPIES)),
+        pltpu.SemaphoreType.DMA((8,)),
+    ]
+
+
+class Scatter:
+    def __init__(self, grads, out, first, p, near, scratch):
+        self.grads, self.out, self.first, self.p, self.near = grads, out, first, p, near
+        self.own, self.other, self.via, self.fin, self.via2, self.fin2, self.last, self.sems, self.local = scratch
+        self.second = "z" if first == "y" else "y"
+        self.copies, self.locals = {}, {}
+
+    def go(self, i, src, dst, to):
+        self.copies[i] = remote(src, dst, self.sems, i, self.near[to])
+        self.copies[i].start()
+
+    def block(self, k, h, core):
+        at = (self.p[self.first] + k) % 4
+        return self.grads.at[:, h, at, core] if self.first == "y" else self.grads.at[at, h, :, core]
+
+    def start(self):
+        for k in ORDER:
+            for h in range(2):
+                i = 2 * k + h
+                self.go(CORE + i, self.block(k, h, 1 - self.p["c"]), self.other.at[k, h], "core")
+                self.locals[i] = pltpu.make_async_copy(
+                    self.block(k, h, self.p["c"]), self.own.at[k, h], self.local.at[i]
+                )
+                self.locals[i].start()
+
+    def paired(self, k):
+        up, down = self.first + "_up", self.first + "_down"
+        for h in range(2):
+            i = 2 * k + h
+            self.copies[CORE + i].wait_recv()
+            self.locals[i].wait()
+
+            def body(s, carry, h=h):
+                self.own[k, h, s] = self.own[k, h, s] + self.other[k, h, s]
+                return carry
+
+            lax.fori_loop(0, 4, body, 0)
+            block = self.own.at[k, h]
+            if k == 2:
+                self.go(VIA + h, block, self.via.at[h], (up, down)[h])
+            elif k == 1 and h == 1:
+                self.go(DIRECT + 1, block, self.fin.at[0, 1], up)
+            elif k == 3 and h == 0:
+                self.go(DIRECT + 2, block, self.fin.at[1, 0], down)
+
+    def relayed(self):
+        for h, k, to, i in ((0, 1, "_up", DIRECT), (1, 3, "_down", DIRECT + 3)):
+            self.copies[VIA + h].wait_recv()
+
+            def body(s, carry, h=h, k=k):
+                self.own[k, h, s] = self.own[k, h, s] + self.via[h, s]
+                return carry
+
+            lax.fori_loop(0, 4, body, 0)
+            self.go(i, self.own.at[k, h], self.fin.at[h, h], self.first + to)
+
+    def first_done(self):
+        m = self.p[self.second]
+        up, down = self.second + "_up", self.second + "_down"
+        for i in range(4):
+            self.copies[DIRECT + i].wait_recv()
+        for k in ORDER:
+            at = (m + k) % 4
+            for h in range(2):
+                self.own[0, h, at] = self.own[0, h, at] + self.fin[0, h, at] + self.fin[1, h, at]
+                block = self.own.at[0, h, at]
+                if k == 2:
+                    self.go(VIA2 + h, block, self.via2.at[h], (up, down)[h])
+                elif k == 1 and h == 1:
+                    self.go(DIRECT2 + 1, block, self.fin2.at[0, 1], up)
+                elif k == 3 and h == 0:
+                    self.go(DIRECT2 + 2, block, self.fin2.at[1, 0], down)
+
+    def relayed2(self):
+        m = self.p[self.second]
+        for h, k, to, i in ((0, 1, "_up", DIRECT2), (1, 3, "_down", DIRECT2 + 3)):
+            at = (m + k) % 4
+            self.copies[VIA2 + h].wait_recv()
+            self.own[0, h, at] = self.own[0, h, at] + self.via2[h]
+            self.go(i, self.own.at[0, h, at], self.fin2.at[h, h], self.second + to)
+
+    def second_done(self):
+        m, x = self.p[self.second], self.p["x"]
+        for i in range(4):
+            self.copies[DIRECT2 + i].wait_recv()
+        for h in range(2):
+            self.own[0, h, m] = self.own[0, h, m] + self.fin2[0, h] + self.fin2[1, h]
+        self.go(LAST, self.own.at[0, 1 - x, m], self.last, "x")
+
+    def finish(self):
+        m, x = self.p[self.second], self.p["x"]
+        self.copies[LAST].wait_recv()
+        self.out[...] = self.own[0, x, m] + self.last[...]
+        for copy in self.copies.values():
+            copy.wait_send()
+
+
+SCATTER_REFS = len(scatter_scratch(128))
+
+
+def small_scratch(rows, both):
+    return [
+        pltpu.VMEM((both, 128), jnp.float32),
+        pltpu.VMEM((3, rows, 128), jnp.float32),
+        pltpu.VMEM((2, rows, 128), jnp.float32),
+        pltpu.VMEM((4, rows, 128), jnp.float32),
+        pltpu.VMEM((4, rows, 128), jnp.float32),
+        pltpu.SemaphoreType.DMA((2, 9)),
+    ]
+
+
+SMALL_REFS = len(small_scratch(8, 8))
+
+
+class SmallSums:
+    def __init__(self, rows, out, p, near, scratch):
+        self.rows, self.out, self.p, self.near = rows, out, p, near
+        self.from_partner, self.held, self.pair, self.along_y, self.along_z, self.sems = scratch
+        self.both = self.from_partner.shape[0]
+        self.copies = []
+
+    def go(self, i, src, dst, to):
+        copy = remote(src, dst, self.sems, i, self.near[to])
+        copy.start()
+        self.copies.append(copy)
+
+    def start(self):
+        self.go(0, self.rows.at[pl.ds(0, self.both)], self.from_partner, "partner")
+
+    def to_core(self):
+        self.copies[0].wait_recv()
+        self.held[0] = self.rows[...]
+        self.held[0, pl.ds(0, self.both)] = self.rows[pl.ds(0, self.both)] + self.from_partner[...]
+        self.go(1, self.held.at[0], self.pair.at[0], "core")
+
+    def to_x(self):
+        self.copies[1].wait_recv()
+        self.held[1] = self.held[0] + self.pair[0]
+        self.go(2, self.held.at[1], self.pair.at[1], "x")
+
+    def ring(self, axis, line, first):
+        for i, name in enumerate(("_up", "_far", "_down")):
+            self.go(first + i, line.at[self.p[axis]], line.at[self.p[axis]], axis + name)
+
+    def to_y(self):
+        self.copies[2].wait_recv()
+        self.along_y[self.p["y"]] = self.held[1] + self.pair[1]
+        self.ring("y", self.along_y, 3)
+
+    def to_z(self):
+        for i in range(3, 6):
+            self.copies[i].wait_recv()
+        a = self.along_y
+        self.along_z[self.p["z"]] = a[0] + a[1] + a[2] + a[3]
+        self.ring("z", self.along_z, 6)
+
+    def finish(self):
+        for i in range(6, 9):
+            self.copies[i].wait_recv()
+        a = self.along_z
+        self.out[...] = a[0] + a[1] + a[2] + a[3]
+        for copy in self.copies:
+            copy.wait_send()
+
+
+def reduce_kernel(firsts, has_small, *refs):
+    refs = list(refs)
+
+    def take(count):
+        taken, refs[:] = refs[:count], refs[count:]
+        return taken
+
+    (terms_ref,), grads = take(1), take(len(firsts))
+    rows = take(1) if has_small else []
+    (theirs_ref,), outs = take(1), take(len(firsts))
+    sums = take(1) if has_small else []
+    p = place()
+    near = neighbours(p)
+    swap_sems = take(1)[0]
+    scatters = [Scatter(g, o, f, p, near, take(SCATTER_REFS)) for g, o, f in zip(grads, outs, firsts)]
+    small = SmallSums(rows[0], sums[0], p, near, take(SMALL_REFS)) if has_small else None
+    names = ["partner", "core", "x", "y_up", "y_down", "z_up", "z_down"]
+    if has_small:
+        names += ["y_far", "z_far"]
+    greet([near[name] for name in names])
+    if has_small:
+        small.start()
+    swap = remote(terms_ref, theirs_ref, swap_sems, 0, near["partner"])
+    swap.start()
+    for s in scatters:
+        s.start()
+    beside = ["to_core", "to_x", "to_y", "to_z"]
+    for k in ORDER:
+        for s in scatters:
+            s.paired(k)
+        if has_small:
+            getattr(small, beside.pop(0))()
+    for name in ("relayed", "first_done", "relayed2", "second_done", "finish"):
+        for s in scatters:
+            getattr(s, name)()
+    if has_small:
+        small.finish()
+    swap.wait()
+
+
+def exchange_and_reduce(terms, grads, firsts, collective_id, rows=None, both=0):
+    f32 = jnp.float32
+    args = [terms] + [g.reshape(4, 2, 4, 2, 16, g.shape[1]) for g in grads]
+    in_specs = [IN_PLACE] * len(args)
+    out_shape = [jax.ShapeDtypeStruct(terms.shape, f32)]
+    out_shape += [jax.ShapeDtypeStruct((16, g.shape[1]), f32) for g in grads]
+    out_specs = [IN_PLACE] + [IN_VMEM] * len(grads)
+    scratch = [pltpu.SemaphoreType.DMA((2, 1))]
+    for g in grads:
+        scratch += scatter_scratch(g.shape[1])
+    if rows is not None:
+        args.append(rows)
+        in_specs.append(IN_VMEM)
+        out_shape.append(jax.ShapeDtypeStruct(rows.shape, f32))
+        out_specs.append(IN_VMEM)
+        scratch += small_scratch(rows.shape[0], both)
+    return pl.pallas_call(
+        functools.partial(reduce_kernel, firsts, rows is not None),
+        out_shape=out_shape,
+        in_specs=in_specs,
+        out_specs=out_specs,
+        scratch_shapes=scratch,
+        compiler_params=pltpu.CompilerParams(
+            collective_id=collective_id, has_side_effects=True, vmem_limit_bytes=60 * 1024 * 1024
+        ),
+    )(*args)
+
+
+def from_partner(value):
+    return lax.ppermute(value, "tensor", [(0, 1), (1, 0)])
 
 
 def layer_norm(values, gain, shift):
@@ -61,12 +320,11 @@
 
 def norm_backward(grad_out, normed, inverse, gain):
     scaled = grad_out * gain
-    grad_rows = inverse * (
+    return inverse * (
         scaled
         - jnp.mean(scaled, axis=-1, keepdims=True)
         - normed * jnp.mean(scaled * normed, axis=-1, keepdims=True)
     )
-    return (grad_rows, jnp.sum(grad_out * normed, axis=0), jnp.sum(grad_out, axis=0))
 
 
 def gelu_parts(inner):
@@ -164,30 +422,35 @@
     allowed = allowed_mask(segment_ids.reshape(seq_count, SEQ))
     attended, log_total = attend_forward(query, keys, values, allowed)
     attended_flat = attended.reshape(tok_rows, local_width)
-    attn_total = taken_together(fdot(attended_flat, w_out), "tensor")
-    middle = inputs + attn_total + b_out
+    attn_terms = fdot(attended_flat, w_out)
+    middle = inputs + (attn_terms + from_partner(attn_terms)) + b_out
     second_f, normed_two, inverse_two = layer_norm(middle, ln_two_gain, ln_two_bias)
     second_in = second_f.astype(jnp.bfloat16)
     inner = fdot(second_in, w_fc) + b_fc
     activated_f, slope = gelu_parts(inner)
     activated = activated_f.astype(jnp.bfloat16)
-    mlp_total = taken_together(fdot(activated, w_proj), "tensor")
-    block_out = middle + mlp_total + b_proj
     top_grad = cotangent.astype(jnp.bfloat16)
     grad_b_proj = jnp.sum(cotangent, axis=0)
-    grad_proj = contract_rows(activated, top_grad)
     grad_inner = contract_cols(top_grad, w_proj) * slope
     grad_b_fc = jnp.sum(grad_inner, axis=0)
     grad_inner_b = grad_inner.astype(jnp.bfloat16)
+    grad_proj = contract_rows(top_grad, activated)
     grad_fc = contract_rows(second_in, grad_inner_b)
-    grad_second = taken_together(contract_cols(grad_inner_b, w_fc), "tensor")
-    rows_two, grad_ln_two_gain, grad_ln_two_bias = norm_backward(
-        grad_second, normed_two, inverse_two, ln_two_gain
-    )
+    second_terms = contract_cols(grad_inner_b, w_fc)
+    second_theirs, proj_share, fc_share = exchange_and_reduce(
+        second_terms, (grad_proj, grad_fc), ("y", "z"), 1
+    )
+    activated_later, second_theirs = lax.optimization_barrier((activated, second_theirs))
+    mlp_terms = fdot(activated_later, w_proj)
+    block_out = middle + (mlp_terms + from_partner(mlp_terms)) + b_proj
+    grad_second = second_terms + second_theirs
+    rows_two = norm_backward(grad_second, normed_two, inverse_two, ln_two_gain)
+    grad_ln_two_gain = jnp.sum(grad_second * normed_two, axis=0)
+    grad_ln_two_bias = jnp.sum(grad_second, axis=0)
     grad_middle = cotangent + rows_two
     grad_b_out = jnp.sum(grad_middle, axis=0)
     middle_b = grad_middle.astype(jnp.bfloat16)
-    grad_w_out = contract_rows(attended_flat, middle_b)
+    grad_w_out = contract_rows(middle_b, attended_flat)
     grad_attended = contract_cols(middle_b, w_out).astype(jnp.bfloat16)
     grad_q, grad_k, grad_v = attend_backward(
         query, keys, values, allowed, log_total, split_heads(grad_attended)
@@ -208,46 +471,46 @@
         + contract_cols(grad_k_b, w_key)
         + contract_cols(grad_v_b, w_value)
     )
-    grad_first = taken_together(first_terms, "tensor")
-    rows_one, grad_ln_one_gain, grad_ln_one_bias = norm_backward(
-        grad_first, normed_one, inverse_one, ln_one_gain
-    )
-    input_grad = grad_middle + rows_one
-    query_share, key_share, value_share, out_share, fc_share, proj_share = sum_together(
-        (grad_query, grad_key, grad_value, grad_w_out, grad_fc, grad_proj), "dp", (0, 0, 0, 1, 0, 1)
-    )
-    small = packed_total(
-        (
-            grad_ln_one_gain,
-            grad_ln_one_bias,
-            grad_b_query,
-            grad_b_value,
-            grad_b_out,
-            grad_ln_two_gain,
-            grad_ln_two_bias,
-            grad_b_fc,
-            grad_b_proj,
-        ),
-        "dp",
-    )
+    small = (
+        jnp.sum(first_terms * normed_one, axis=0),
+        jnp.sum(first_terms, axis=0),
+        grad_b_query,
+        grad_b_value,
+        grad_b_out,
+        grad_ln_two_gain,
+        grad_ln_two_bias,
+        grad_b_fc,
+        grad_b_proj,
+    )
+    rows = jnp.concatenate([part.reshape(-1, 128) for part in small], axis=0)
+    both = (small[0].size + small[1].size) // 128
+    first_theirs, query_share, key_share, value_share, out_share, sums = exchange_and_reduce(
+        first_terms, (grad_query, grad_key, grad_value, grad_w_out), ("y", "y", "z", "z"), 2, rows, both
+    )
+    input_grad = grad_middle + norm_backward(first_terms + first_theirs, normed_one, inverse_one, ln_one_gain)
+    totals, at = [], 0
+    for part in small:
+        count = part.size // 128
+        totals.append(sums[at : at + count].reshape(-1))
+        at += count
     return (
         block_out,
         input_grad,
-        small[0],
-        small[1],
+        totals[0],
+        totals[1],
         query_share,
         key_share,
         value_share,
-        small[2],
-        small[3],
-        out_share,
-        small[4],
-        small[5],
-        small[6],
+        totals[2],
+        totals[3],
+        out_share.T,
+        totals[4],
+        totals[5],
+        totals[6],
         fc_share,
-        small[7],
-        proj_share,
-        small[8],
+        totals[7],
+        proj_share.T,
+        totals[8],
     )
 
 

time: 771 us -> 376 us (0.49)
  waiting for transfers between devices: 316 us -> 90.4 us
  local copies, waits for them, and re-layouts: 175 us -> 19.6 us
  Pallas kernels: 0 us -> 143 us
  blocking collectives: 111 us -> 0 us
  other arithmetic: 32.4 us -> 16.7 us
  between operations: 14.9 us -> 1.48 us
  matrix products: 94.8 us -> 86.2 us
    reduce_scatter x1 -> x0, waiting for transfers between devices: 207 us -> none  [sum_together(): lax.psum_scatter(lines, axis, tiled=True).reshape(-1)]
    pallas_call x0 -> x2, Pallas kernels: none -> 143 us  [exchange_and_reduce(): pl.pallas_call(functools.partial(reduce_kernel, firsts, rows is not None)...]
    all_to_all x2 -> x0, blocking collectives: 111 us -> none  [from_everyone(): lax.all_to_all(jnp.broadcast_to(value[None], (devices, *value.shape)), ax...]
    all_to_all x3 -> x0, waiting for transfers between devices: 109 us -> none  [from_everyone(): lax.all_to_all(jnp.broadcast_to(value[None], (devices, *value.shape)), ax...]
    ppermute x0 -> x2, waiting for transfers between devices: none -> 90.4 us  [from_partner(): return lax.ppermute(value, 'tensor', [(0, 1), (1, 0)])]
    concatenate x3 -> x1, local copies, waits for them, and re-layouts: 42.4 us -> 4.76 us  [on_device(): rows = jnp.concatenate([part.reshape(-1, 128) for part in small], axis=0)]
    another operation x8 -> x0, local copies, waits for them, and re-layouts: 35.4 us -> none  [sum_together(): lines = jnp.concatenate([b.reshape(devices, -1) for b in blocks], axis=1)]
    reshape x8 -> x5, local copies, waits for them, and re-layouts: 37.5 us -> 4.11 us  [the longest x3 3.96 us: on_device(): totals.append(sums[at:at + count].reshape(-1))]
  transfers between devices with their start and end apart: 4 -> 2, of which waited for: 3 -> 2; matrix products, arithmetic and copies ran while one was open for 10% -> 0% of each run, Pallas kernels for 0% -> 0%
where the time goes in v1:
time: 376 us; the launch traced here: 372 us
  Pallas kernels  143 us (38%)
  waiting for transfers between devices  90.4 us (24%)
  matrix products  86.2 us (23%)
  local copies, waits for them, and re-layouts  19.6 us (5%)
  other arithmetic  16.7 us (4%)
  starting transfers between devices  15.2 us (4%)
    pallas_call x2, Pallas kernels, exchange_and_reduce(): pl.pallas_call(functools.partial(reduce_kernel, firsts, rows is not None)...  143 us
    ppermute x2, waiting for transfers between devices, from_partner(): return lax.ppermute(value, 'tensor', [(0, 1), (1, 0)])  90.4 us
    dot_general x6, matrix products, contract_rows(): jnp.einsum('ta,tb->ab', left, right, preferred_element_type=jnp.float32)  20.8 us
    ppermute x2, starting transfers between devices, from_partner(): return lax.ppermute(value, 'tensor', [(0, 1), (1, 0)])  15.2 us
    dot_general x1, matrix products, attend_backward(): jnp.einsum('bhqk,bqhd->bkhd', grad_scores, query, preferred_element_type=...  14.3 us
    dot_general x1, matrix products, attend_backward(): jnp.einsum('bhqk,bkhd->bqhd', grad_scores, keys, preferred_element_type=j...  14.2 us
    dot_general x6, matrix products, contract_cols(): jnp.einsum('ta,ba->tb', left, right, preferred_element_type=jnp.float32)  13 us
    dot_general x6, matrix products, fdot(): return jnp.dot(left, right, preferred_element_type=jnp.float32)  12.4 us
  transfers between devices with their start and end apart: 2, of which 2 were waited for; matrix products, arithmetic and copies ran while one was open for 0% of the time, Pallas kernels for 0%

profile of v1, /device:TPU:0, one launch (start us, length us, event | category | flops | bytes accessed | tf_op | source)
XLA Modules:
  0.0 372.3 jit_solution(12866237210812076409)
XLA Ops:
  11.2 2.4 convolution_convert_fusion
  14.3 3.5 collective-permute-start
  17.8 45.6 %collective-permute-done = f32[512,1024]{1,0:T(8,128)S(1)} collective-permute-done((f32[512,1024]{1,0:T(8,128)S(1)}, f32[512,1024]{1,0:T(8,128)S(1)}, u32[]{:S(2)}, u32[]{:S(2)}) %collective-permute-start) | collective-permute-done | bytes 2097184 | tf_op jit(solution)/shard_map/ppermute | solution.py:311
  66.4 3.4 multiply_convert_fusion.1
  69.9 4.8 %fusion.92 = (f32[2048]{0:T(1024)S(1)}, bf16[512,2048]{1,0:T(8,128)(2,1)S(1)}) fusion(f32[512,2048]{1,0:T(8,128)S(1)} %get-tuple-element.71, f32[2048]{0:T(1024)S(1)} %copy-done.41, bf16[2048,1024]{1,0:T(8,128)(2,1)S(1)} %copy-done.40, f32[512,1024]{1,0:T(8,128)S(1)} %copy-done.9), kind=kOutput, calls=%fused_computation.109 | convolution fusion | flops 2170025984 | bytes 12599296 | tf_op jit(solution)/shard_map/ta,ba->tb/dot_general | solution.py:348
  74.7 3.7 fusion.59.refs_0_
  78.4 5.9 %fusion.57 = f32[1024,2048]{1,0:T(8,128)} fusion(bf16[512,2048]{1,0:T(8,128)(2,1)S(1)} %get-tuple-element.75, f32[512,1024]{1,0:T(8,128)S(1)} %get-tuple-element.52, f32[1024]{0:T(1024)S(1)} %copy-done.42, f32[1024]{0:T(1024)S(1)} %copy-done.34, f32[512]{0:T(512)S(1)} %add_rsqrt_fusion, f32[512]{0:T(512)S(1)} %broadcast_multiply_fusion.4), kind=kOutput, calls=%fused_computation.66 | convolution fusion | flops 2150105088 | bytes 12595200 | tf_op jit(solution)/shard_map/ta,tb->ab/dot_general | solution.py:344
  84.3 5.6 %fusion.63 = f32[2048,1024]{0,1:T(8,128)} fusion(bf16[512,2048]{1,0:T(8,128)(2,1)S(1)} %get-tuple-element.29, f32[512,1024]{1,0:T(8,128)S(1)} %copy-done.9), kind=kOutput, calls=%fused_computation.74 | convolution fusion | flops 2148007936 | bytes 12582912 | tf_op jit(solution)/shard_map/ta,tb->ab/dot_general | solution.py:344
  89.9 66.0 %shard_map.305 = (f32[512,1024]{1,0:T(8,128)}, f32[16,2048]{1,0:T(8,128)}, f32[16,2048]{1,0:T(8,128)}) custom-call(f32[512,1024]{1,0:T(8,128)} %fusion.59.refs_0_, f32[4,2,4,2,16,2048]{5,4,3,2,1,0:T(8,128)} %bitcast.107, f32[4,2,4,2,16,2048]{5,4,3,2,1,0:T(8,128)} %bitcast.111), custom_call_target="tpu_custom_call" | custom-call | tf_op jit(solution)/shard_map/pallas_call | solution.py:298
  155.9 5.3 %fusion.94 = f32[512,1024]{1,0:T(8,128)S(1)} fusion(bf16[512,2048]{1,0:T(8,128)(2,1)} %copy-done.18, bf16[2048,1024]{1,0:T(8,128)(2,1)} %param.33), kind=kOutput, calls=%fused_computation.111 | convolution fusion | flops 2147483648 | bytes 8388608 | tf_op jit(solution)/shard_map/dot_general | solution.py:340
  161.2 11.8 %collective-permute-start.1 = (f32[512,1024]{1,0:T(8,128)S(1)}, f32[512,1024]{1,0:T(8,128)S(1)}, u32[]{:S(2)}, u32[]{:S(2)}) collective-permute-start(f32[512,1024]{1,0:T(8,128)S(1)} %fusion.94), channel_id=1, source_target_pairs={{0,1},{1,0},{2,3},{3,2},{4,5},{5,4},{6,7},{7,6},{8,9},{9,8},{10,11... | collective-permute-start | bytes 6291464 | tf_op jit(solution)/shard_map/ppermute | solution.py:311
  174.4 44.8 %collective-permute-done.1 = f32[512,1024]{1,0:T(8,128)S(1)} collective-permute-done((f32[512,1024]{1,0:T(8,128)S(1)}, f32[512,1024]{1,0:T(8,128)S(1)}, u32[]{:S(2)}, u32[]{:S(2)}) %collective-permute-start.1) | collective-permute-done | bytes 2097184 | tf_op jit(solution)/shard_map/ppermute | solution.py:311
  219.2 2.3 fusion.85
  222.8 3.1 fusion.88
  225.9 4.5 %fusion.95 = f32[8,512,512]{1,2,0:T(8,128)} fusion(bf16[512,8,64]{0,2,1:T(8,128)(2,1)S(1)} %bitcast.120, bf16[512,8,64]{0,2,1:T(8,128)(2,1)S(1)} %bitcast.128), kind=kOutput, calls=%fused_computation.112 | convolution fusion | flops 268435456 | bytes 9437184 | tf_op jit(solution)/shard_map/bqhd,bkhd->bhqk/dot_general | solution.py:377
  230.4 14.3 %fusion.54 = bf16[8,64,512]{2,1,0:T(8,128)(2,1)} fusion(bf16[512,8,64]{0,2,1:T(8,128)(2,1)} %bitcast.126, f32[8,512,512]{1,2,0:T(8,128)} %fusion.95, f32[8,512,512]{1,2,0:T(8,128)} %copy-done.2, f32[8,512]{1,0:T(8,128)S(1)} %log_add_fusion, pred[512,512]{0,1:T(8,128)(4,1)S(1)} %fusion.61), kind=kOutput, calls=%fused_computation.63 | convolution fusion | flops 291770880 | bytes 18104320 | tf_op jit(solution)/shard_map/bhqk,bqhd->bkhd/dot_general | solution.py:383
  244.7 14.2 %fusion.89 = (f32[8,64]{1,0:T(8,128)S(1)}, bf16[1,512,8,64]{1,3,2,0:T(8,128)(2,1)}) fusion(bf16[512,8,64]{0,2,1:T(8,128)(2,1)} %bitcast.124, f32[8,512,512]{1,2,0:T(8,128)} %fusion.95, f32[8,512,512]{1,2,0:T(8,128)} %copy-done.2, f32[8,512]{1,0:T(8,128)S(1)} %log_add_fusion, pred[512,512]{0,1:T(8,128)(4,1)S(1)} %fusion.61), kind=kOutput, calls=%fused_computation.108 | convolution fusion | flops 292032512 | bytes 18106368 | tf_op jit(solution)/shard_map/bhqk,bkhd->bqhd/dot_general | solution.py:382
  260.7 2.2 fusion.97
  268.2 3.1 fusion.100.refs_3_
  273.5 2.1 fusion.98.refs_1_
  275.5 2.1 fusion.101.refs_4_
  277.6 4.8 %concatenate.3.refs_5_ = f32[72,128]{1,0:T(8,128)} concatenate(f32[8,128]{1,0:T(8,128)S(1)} %bitcast.134, f32[8,128]{1,0:T(8,128)S(1)} %bitcast.133, f32[4,128]{1,0:T(4,128)S(1)} %reshape.308, f32[4,128]{1,0:T(4,128)S(1)} %reshape.309, f32[8,128]{1,0:T(8,128)S(1)} %bitcast.135, f32[8,128]{1,0:T(8,128)S(1)} %bitcast.131, f32[8,128]{1,0:T(8,128)S(1)} %bitcast.132, ...), dimensions={0} | concatenate | bytes 73728 | tf_op jit(solution)/shard_map/concatenate | solution.py:485
  282.3 76.7 %shard_map.306 = (f32[512,1024]{1,0:T(8,128)}, f32[16,512]{1,0:T(8,128)}, f32[16,512]{1,0:T(8,128)}, f32[16,512]{1,0:T(8,128)}, f32[16,512]{1,0:T(8,128)}, /*index=5*/f32[72,128]{1,0:T(8,128)}) custom-call(f32[512,1024]{1,0:T(8,128)} %copy-done.5, f32[4,2,4,2,16,512]{5,4,3,2,1,0:T(8,128)} %fusion.98.refs_1_, f32[4,2,4,2,16,512]{5,4,3,2,1,0:T(8,128)} %fusion.99.refs_2_, ...), custom_call_target="tpu_custom_call" | custom-call | tf_op jit(solution)/shard_map/pallas_call | solution.py:298
  363.0 3.2 fusion.83
  (135 shorter events, 35.5 us)
Async XLA Ops:
  0.7 12.9 %copy-start = (bf16[512,1024]{1,0:T(8,128)(2,1)S(1)}, bf16[512,1024]{1,0:T(8,128)(2,1)}, u32[]{:S(2)}) copy-start(bf16[512,1024]{1,0:T(8,128)(2,1)} %param.27) | copy-start | bytes 3145732
  0.7 3.5 copy-start.1
  0.7 3.3 copy-start.35
  0.7 3.5 copy-start.33
  0.7 3.5 copy-start.37
  0.7 3.5 copy-start.20
  13.6 50.4 %copy-start.12 = (bf16[8,64,512]{2,1,0:T(8,128)(2,1)}, bf16[8,64,512]{2,1,0:T(8,128)(2,1)S(1)}, u32[]{:S(2)}) copy-start(bf16[8,64,512]{2,1,0:T(8,128)(2,1)S(1)} %convolution_convert_fusion) | copy-start | bytes 1572868
  13.6 49.9 %copy-start.36 = (f32[1024]{0:T(1024)S(1)}, f32[1024]{0:T(1024)}, u32[]{:S(2)}) copy-start(f32[1024]{0:T(1024)} %param.28) | copy-start | bytes 12292
  14.3 49.1 %collective-permute-start = (f32[512,1024]{1,0:T(8,128)S(1)}, f32[512,1024]{1,0:T(8,128)S(1)}, u32[]{:S(2)}, u32[]{:S(2)}) collective-permute-start(f32[512,1024]{1,0:T(8,128)S(1)} %fusion.93), channel_id=1, source_target_pairs={{0,1},{1,0},{2,3},{3,2},{4,5},{5,4},{6,7},{7,6},{8,9},{9,8},{10,11... | collective-permute-start | bytes 6291464 | tf_op jit(solution)/shard_map/ppermute | solution.py:311
  63.9 14.5 %copy-start.6 = (f32[512,1024]{1,0:T(8,128)}, f32[512,1024]{1,0:T(8,128)S(1)}, u32[]{:S(2)}) copy-start(f32[512,1024]{1,0:T(8,128)S(1)} %get-tuple-element.52) | copy-start | bytes 6291460
  66.4 3.5 copy-start.9
  66.4 3.5 copy-start.40
  69.9 14.4 %copy-start.18 = (bf16[512,2048]{1,0:T(8,128)(2,1)}, bf16[512,2048]{1,0:T(8,128)(2,1)S(1)}, u32[]{:S(2)}) copy-start(bf16[512,2048]{1,0:T(8,128)(2,1)S(1)} %get-tuple-element.29) | copy-start | bytes 6291460
  155.9 17.1 %copy-start.7 = (f32[512,1024]{1,0:T(8,128)S(1)}, f32[512,1024]{1,0:T(8,128)}, u32[]{:S(2)}) copy-start(f32[512,1024]{1,0:T(8,128)} %copy-done.6) | copy-start | bytes 6291460
  155.9 17.1 %copy-start.8 = (f32[512,1024]{1,0:T(8,128)S(1)}, f32[512,1024]{1,0:T(8,128)}, u32[]{:S(2)}) copy-start(f32[512,1024]{1,0:T(8,128)} %fusion.59.refs_0_) | copy-start | bytes 6291460
  155.9 17.1 %copy-start.17 = (f32[512,1024]{1,0:T(8,128)S(1)}, f32[512,1024]{1,0:T(8,128)}, u32[]{:S(2)}) copy-start(f32[512,1024]{1,0:T(8,128)} %get-tuple-element.30) | copy-start | bytes 6291460
  161.2 57.9 %collective-permute-start.1 = (f32[512,1024]{1,0:T(8,128)S(1)}, f32[512,1024]{1,0:T(8,128)S(1)}, u32[]{:S(2)}, u32[]{:S(2)}) collective-permute-start(f32[512,1024]{1,0:T(8,128)S(1)} %fusion.94), channel_id=1, source_target_pairs={{0,1},{1,0},{2,3},{3,2},{4,5},{5,4},{6,7},{7,6},{8,9},{9,8},{10,11... | collective-permute-start | bytes 6291464 | tf_op jit(solution)/shard_map/ppermute | solution.py:311
  173.0 46.2 %copy-start.10 = (f32[512,1024]{1,0:T(8,128)S(1)}, f32[512,1024]{1,0:T(8,128)}, u32[]{:S(2)}) copy-start(f32[512,1024]{1,0:T(8,128)} %param.35) | copy-start | bytes 6291460
  173.0 46.2 %copy-start.38 = (f32[1024]{0:T(1024)S(1)}, f32[1024]{0:T(1024)}, u32[]{:S(2)}) copy-start(f32[1024]{0:T(1024)} %param.34) | copy-start | bytes 12292
  173.0 49.8 %slice-start = ((s8[8388608]{0:T(1024)(128)(4,1)}), s8[4194304]{0:T(1024)(128)(4,1)S(1)}, s32[]{:S(2)}) async-start(s8[8388608]{0:T(1024)(128)(4,1)} %bitcast.105), calls=%async_computation | async-start | bytes 8388608
  219.2 3.6 slice-start.1
  366.3 3.9 %copy-start.29 = (f32[16,512]{1,0:T(8,128)S(1)}, f32[16,512]{1,0:T(8,128)}, u32[]{:S(2)}) copy-start(f32[16,512]{1,0:T(8,128)} %get-tuple-element.36) | copy-start | bytes 98308
  366.3 4.5 %copy-start.28 = (f32[16,2048]{1,0:T(8,128)S(1)}, f32[16,2048]{1,0:T(8,128)}, u32[]{:S(2)}) copy-start(f32[16,2048]{1,0:T(8,128)} %get-tuple-element.110) | copy-start | bytes 393220
  366.3 5.1 %copy-start.27 = (f32[16,2048]{1,0:T(8,128)S(1)}, f32[16,2048]{1,0:T(8,128)}, u32[]{:S(2)}) copy-start(f32[16,2048]{1,0:T(8,128)} %get-tuple-element.38) | copy-start | bytes 393220
  (25 other events, 53.0 us)

commit v2 on v1

--- a/solution.py
+++ b/solution.py
@@ -177,7 +177,7 @@
 def small_scratch(rows, both):
     return [
         pltpu.VMEM((both, 128), jnp.float32),
-        pltpu.VMEM((3, rows, 128), jnp.float32),
+        pltpu.VMEM((2, rows, 128), jnp.float32),
         pltpu.VMEM((2, rows, 128), jnp.float32),
         pltpu.VMEM((4, rows, 128), jnp.float32),
         pltpu.VMEM((4, rows, 128), jnp.float32),
@@ -209,32 +209,32 @@
         self.held[0, pl.ds(0, self.both)] = self.rows[pl.ds(0, self.both)] + self.from_partner[...]
         self.go(1, self.held.at[0], self.pair.at[0], "core")
 
-    def to_x(self):
-        self.copies[1].wait_recv()
-        self.held[1] = self.held[0] + self.pair[0]
-        self.go(2, self.held.at[1], self.pair.at[1], "x")
-
     def ring(self, axis, line, first):
         for i, name in enumerate(("_up", "_far", "_down")):
             self.go(first + i, line.at[self.p[axis]], line.at[self.p[axis]], axis + name)
 
     def to_y(self):
-        self.copies[2].wait_recv()
-        self.along_y[self.p["y"]] = self.held[1] + self.pair[1]
-        self.ring("y", self.along_y, 3)
+        self.copies[1].wait_recv()
+        self.along_y[self.p["y"]] = self.held[0] + self.pair[0]
+        self.ring("y", self.along_y, 2)
 
     def to_z(self):
-        for i in range(3, 6):
+        for i in range(2, 5):
             self.copies[i].wait_recv()
         a = self.along_y
         self.along_z[self.p["z"]] = a[0] + a[1] + a[2] + a[3]
-        self.ring("z", self.along_z, 6)
-
-    def finish(self):
-        for i in range(6, 9):
+        self.ring("z", self.along_z, 5)
+
+    def to_x(self):
+        for i in range(5, 8):
             self.copies[i].wait_recv()
         a = self.along_z
-        self.out[...] = a[0] + a[1] + a[2] + a[3]
+        self.held[1] = a[0] + a[1] + a[2] + a[3]
+        self.go(8, self.held.at[1], self.pair.at[1], "x")
+
+    def finish(self):
+        self.copies[8].wait_recv()
+        self.out[...] = self.held[1] + self.pair[1]
         for copy in self.copies:
             copy.wait_send()
 
@@ -265,7 +265,7 @@
     swap.start()
     for s in scatters:
         s.start()
-    beside = ["to_core", "to_x", "to_y", "to_z"]
+    beside = ["to_core", "to_y", "to_z", "to_x"]
     for k in ORDER:
         for s in scatters:
             s.paired(k)
@@ -348,41 +348,127 @@
     return jnp.einsum("ta,ba->tb", left, right, preferred_element_type=jnp.float32)
 
 
-def allowed_mask(segments):
-    rows = lax.broadcasted_iota(jnp.int32, (SEQ, SEQ), 0)
-    cols = lax.broadcasted_iota(jnp.int32, (SEQ, SEQ), 1)
-    same = segments[:, :, None] == segments[:, None, :]
-    return (same & (cols <= rows)[None])[:, None]
-
-
-def masked_scores(query, keys, allowed):
-    scale = 1.0 / HEAD_DIM**0.5
-    scores = jnp.einsum("bqhd,bkhd->bhqk", query, keys, preferred_element_type=jnp.float32) * scale
-    return jnp.where(allowed, scores, -1e30)
-
-
-def attend_forward(query, keys, values, allowed):
-    masked = masked_scores(query, keys, allowed)
-    top = jnp.max(masked, axis=-1, keepdims=True)
-    log_total = top + jnp.log(jnp.sum(jnp.exp(masked - top), axis=-1, keepdims=True))
-    probs = jnp.exp(masked - log_total).astype(jnp.bfloat16)
-    attended = jnp.einsum("bhqk,bkhd->bqhd", probs, values, preferred_element_type=jnp.float32)
-    return (attended.astype(jnp.bfloat16), log_total)
-
-
-def attend_backward(query, keys, values, allowed, log_total, grad_attended):
-    scale = 1.0 / HEAD_DIM**0.5
-    probs_f = jnp.exp(masked_scores(query, keys, allowed) - log_total)
-    probs = probs_f.astype(jnp.bfloat16)
-    grad_probs = jnp.einsum(
-        "bqhd,bkhd->bhqk", grad_attended, values, preferred_element_type=jnp.float32
-    )
-    delta = jnp.sum(probs_f * grad_probs, axis=-1, keepdims=True)
-    grad_scores = (probs_f * (grad_probs - delta) * scale).astype(jnp.bfloat16)
-    grad_q = jnp.einsum("bhqk,bkhd->bqhd", grad_scores, keys, preferred_element_type=jnp.float32)
-    grad_k = jnp.einsum("bhqk,bqhd->bkhd", grad_scores, query, preferred_element_type=jnp.float32)
-    grad_v = jnp.einsum("bhqk,bqhd->bkhd", probs, grad_attended, preferred_element_type=jnp.float32)
-    return (grad_q, grad_k, grad_v)
+BLOCK = 256
+SCALE = 1.0 / HEAD_DIM**0.5
+
+
+def dot_over(left, right, left_dim, right_dim):
+    return lax.dot_general(
+        left, right, (((left_dim,), (right_dim,)), ((), ())), preferred_element_type=jnp.float32
+    )
+
+
+def mask_tokens(column_ref, row_ref, mask_ref):
+    u = lax.broadcasted_iota(jnp.int32, (SEQ, SEQ), 0)
+    t = lax.broadcasted_iota(jnp.int32, (SEQ, SEQ), 1)
+    allowed = (column_ref[...] == row_ref[...]) & (u <= t)
+    mask_ref[...] = jnp.where(allowed, 0.0, -1e30)
+
+
+def blocks_of_tokens():
+    for at in range(0, SEQ, BLOCK):
+        yield slice(at, at + BLOCK), at + BLOCK
+
+
+def attend_kernel(q_ref, k_ref, v_ref, column_ref, row_ref, out_ref, log_ref, mask_ref):
+    mask_tokens(column_ref, row_ref, mask_ref)
+
+    def two_heads(i, carry):
+        cols = pl.ds(pl.multiple_of(i * 2 * HEAD_DIM, 2 * HEAD_DIM), 2 * HEAD_DIM)
+        halves = []
+        for h in range(2):
+            e = slice(h * HEAD_DIM, (h + 1) * HEAD_DIM)
+            q, k, v = q_ref[:, cols][:, e], k_ref[:, cols][:, e], v_ref[:, cols][:, e]
+            rows, logs = [], []
+            for t, end in blocks_of_tokens():
+                scores = dot_over(k[:end], q[t], 1, 1) + mask_ref[:end, t]
+                top = jnp.max(scores, axis=0, keepdims=True)
+                weights = jnp.exp(scores - top)
+                total = jnp.sum(weights, axis=0, keepdims=True)
+                probs = (weights * (1.0 / total)).astype(jnp.bfloat16)
+                logs.append(top + jnp.log(total))
+                rows.append(dot_over(v[:end], probs, 0, 0).T)
+            log_ref[pl.ds(2 * i + h, 1), :] = jnp.concatenate(logs, axis=1)
+            halves.append(jnp.concatenate(rows, axis=0))
+        out_ref[:, cols] = jnp.concatenate(halves, axis=1).astype(jnp.bfloat16)
+        return carry
+
+    lax.fori_loop(0, q_ref.shape[1] // (2 * HEAD_DIM), two_heads, 0)
+
+
+def attend_forward(query, keys, values, column, row):
+    heads = query.shape[1] // HEAD_DIM
+    return pl.pallas_call(
+        attend_kernel,
+        out_shape=[
+            jax.ShapeDtypeStruct(query.shape, jnp.bfloat16),
+            jax.ShapeDtypeStruct((heads, SEQ), jnp.float32),
+        ],
+        in_specs=[IN_VMEM] * 5,
+        out_specs=[IN_VMEM] * 2,
+        scratch_shapes=[pltpu.VMEM((SEQ, SEQ), jnp.float32)],
+        compiler_params=pltpu.CompilerParams(vmem_limit_bytes=32 * 1024 * 1024),
+    )(query, keys, values, column, row)
+
+
+def attend_back_kernel(
+    terms_ref, q_ref, k_ref, v_ref, grad_ref, log_ref, column_ref, row_ref,
+    theirs_ref, gq_ref, gk_ref, gv_ref, bq_ref, bv_ref,
+    mask_ref, sems,
+):
+    partner = neighbours(place())["partner"]
+    greet([partner])
+    swap = remote(terms_ref, theirs_ref, sems, 0, partner)
+    swap.start()
+    mask_tokens(column_ref, row_ref, mask_ref)
+
+    def two_heads(i, carry):
+        cols = pl.ds(pl.multiple_of(i * 2 * HEAD_DIM, 2 * HEAD_DIM), 2 * HEAD_DIM)
+        halves = []
+        for h in range(2):
+            e = slice(h * HEAD_DIM, (h + 1) * HEAD_DIM)
+            q, k, v, g = q_ref[:, cols][:, e], k_ref[:, cols][:, e], v_ref[:, cols][:, e], grad_ref[:, cols][:, e]
+            logs = log_ref[pl.ds(2 * i + h, 1), :]
+            gq, gk, gv = [], None, None
+            for t, end in blocks_of_tokens():
+                scores = dot_over(k[:end], q[t], 1, 1) + mask_ref[:end, t]
+                probs = jnp.exp(scores - logs[:, t])
+                grad_probs = dot_over(v[:end], g[t], 1, 1)
+                delta = jnp.sum(probs * grad_probs, axis=0, keepdims=True)
+                grad_scores = (probs * (grad_probs - delta)).astype(jnp.bfloat16)
+                of_k = dot_over(grad_scores, q[t], 1, 0)
+                of_v = dot_over(probs.astype(jnp.bfloat16), g[t], 1, 0)
+                gq.append(dot_over(k[:end], grad_scores, 0, 0).T * SCALE)
+                if gk is not None:
+                    of_k = jnp.concatenate([gk + of_k[: gk.shape[0]], of_k[gk.shape[0] :]], axis=0)
+                    of_v = jnp.concatenate([gv + of_v[: gv.shape[0]], of_v[gv.shape[0] :]], axis=0)
+                gk, gv = of_k, of_v
+            halves.append((jnp.concatenate(gq, axis=0), gk, gv))
+        gq, gk, gv = (jnp.concatenate(pair, axis=1) for pair in zip(*halves))
+        bq_ref[:, cols] = jnp.sum(gq, axis=0, keepdims=True)
+        bv_ref[:, cols] = jnp.sum(gv, axis=0, keepdims=True)
+        gq_ref[:, cols] = gq.astype(jnp.bfloat16)
+        gk_ref[:, cols] = gk.astype(jnp.bfloat16)
+        gv_ref[:, cols] = gv.astype(jnp.bfloat16)
+        return carry
+
+    lax.fori_loop(0, q_ref.shape[1] // (2 * HEAD_DIM), two_heads, 0)
+    swap.wait()
+
+
+def attend_backward(terms, query, keys, values, grad_attended, logs, column, row, collective_id):
+    grad = jax.ShapeDtypeStruct(query.shape, jnp.bfloat16)
+    total = jax.ShapeDtypeStruct((1, query.shape[1]), jnp.float32)
+    return pl.pallas_call(
+        attend_back_kernel,
+        out_shape=[jax.ShapeDtypeStruct(terms.shape, jnp.float32), grad, grad, grad, total, total],
+        in_specs=[IN_PLACE] + [IN_VMEM] * 7,
+        out_specs=[IN_PLACE] + [IN_VMEM] * 5,
+        scratch_shapes=[pltpu.VMEM((SEQ, SEQ), jnp.float32), pltpu.SemaphoreType.DMA((2, 1))],
+        compiler_params=pltpu.CompilerParams(
+            collective_id=collective_id, has_side_effects=True, vmem_limit_bytes=32 * 1024 * 1024
+        ),
+    )(terms, query, keys, values, grad_attended, logs, column, row)
 
 
 def on_device(
@@ -405,24 +491,15 @@
     b_proj,
     cotangent,
 ):
-    tok_rows = hidden_in.shape[0]
-    seq_count = tok_rows // SEQ
-    local_width = w_query.shape[1]
-    local_heads = local_width // HEAD_DIM
-
-    def split_heads(flat):
-        return flat.reshape(seq_count, SEQ, local_heads, HEAD_DIM)
-
+    column, row = segment_ids.reshape(SEQ, 1), segment_ids.reshape(1, SEQ)
     inputs = hidden_in.astype(jnp.float32)
     first_f, normed_one, inverse_one = layer_norm(inputs, ln_one_gain, ln_one_bias)
     first_in = first_f.astype(jnp.bfloat16)
-    query = split_heads((fdot(first_in, w_query) + b_query).astype(jnp.bfloat16))
-    keys = split_heads(fdot(first_in, w_key).astype(jnp.bfloat16))
-    values = split_heads((fdot(first_in, w_value) + b_value).astype(jnp.bfloat16))
-    allowed = allowed_mask(segment_ids.reshape(seq_count, SEQ))
-    attended, log_total = attend_forward(query, keys, values, allowed)
-    attended_flat = attended.reshape(tok_rows, local_width)
-    attn_terms = fdot(attended_flat, w_out)
+    query = (fdot(first_in, w_query) + b_query).astype(jnp.bfloat16) * jnp.bfloat16(SCALE)
+    keys = fdot(first_in, w_key).astype(jnp.bfloat16)
+    values = (fdot(first_in, w_value) + b_value).astype(jnp.bfloat16)
+    attended, logs = attend_forward(query, keys, values, column, row)
+    attn_terms = fdot(attended, w_out)
     middle = inputs + (attn_terms + from_partner(attn_terms)) + b_out
     second_f, normed_two, inverse_two = layer_norm(middle, ln_two_gain, ln_two_bias)
     second_in = second_f.astype(jnp.bfloat16)
@@ -440,9 +517,6 @@
     second_theirs, proj_share, fc_share = exchange_and_reduce(
         second_terms, (grad_proj, grad_fc), ("y", "z"), 1
     )
-    activated_later, second_theirs = lax.optimization_barrier((activated, second_theirs))
-    mlp_terms = fdot(activated_later, w_proj)
-    block_out = middle + (mlp_terms + from_partner(mlp_terms)) + b_proj
     grad_second = second_terms + second_theirs
     rows_two = norm_backward(grad_second, normed_two, inverse_two, ln_two_gain)
     grad_ln_two_gain = jnp.sum(grad_second * normed_two, axis=0)
@@ -450,19 +524,13 @@
     grad_middle = cotangent + rows_two
     grad_b_out = jnp.sum(grad_middle, axis=0)
     middle_b = grad_middle.astype(jnp.bfloat16)
-    grad_w_out = contract_rows(middle_b, attended_flat)
+    grad_w_out = contract_rows(middle_b, attended)
     grad_attended = contract_cols(middle_b, w_out).astype(jnp.bfloat16)
-    grad_q, grad_k, grad_v = attend_backward(
-        query, keys, values, allowed, log_total, split_heads(grad_attended)
-    )
-    grad_q = grad_q.reshape(tok_rows, local_width)
-    grad_k = grad_k.reshape(tok_rows, local_width)
-    grad_v = grad_v.reshape(tok_rows, local_width)
-    grad_b_query = jnp.sum(grad_q, axis=0)
-    grad_b_value = jnp.sum(grad_v, axis=0)
-    grad_q_b = grad_q.astype(jnp.bfloat16)
-    grad_k_b = grad_k.astype(jnp.bfloat16)
-    grad_v_b = grad_v.astype(jnp.bfloat16)
+    mlp_terms = fdot(activated, w_proj)
+    mlp_theirs, grad_q_b, grad_k_b, grad_v_b, grad_b_query, grad_b_value = attend_backward(
+        mlp_terms, query, keys, values, grad_attended, logs, column, row, 3
+    )
+    block_out = middle + (mlp_terms + mlp_theirs) + b_proj
     grad_query = contract_rows(first_in, grad_q_b)
     grad_key = contract_rows(first_in, grad_k_b)
     grad_value = contract_rows(first_in, grad_v_b)

time: 376 us -> 306 us (0.81)
  waiting for transfers between devices: 90.4 us -> 45.6 us
  matrix products: 86.2 us -> 43.2 us
  Pallas kernels: 143 us -> 179 us
  starting transfers between devices: 15.2 us -> 3.21 us
    pallas_call x0 -> x2, Pallas kernels: none -> 57.1 us  [the longest x1 49.5 us: attend_backward(): pl.pallas_call(attend_back_kernel, out_shape=[jax.ShapeDtypeStruct(terms....]
    ppermute x2 -> x1, waiting for transfers between devices: 90.4 us -> 45.6 us  [from_partner(): return lax.ppermute(value, 'tensor', [(0, 1), (1, 0)])]
    dot_general x6 -> x0, matrix products: 40 us -> none  [the longest x1 14.3 us: attend_backward(): jnp.einsum('bhqk,bqhd->bkhd', grad_scores, query, preferred_element_type=...]
    pallas_call x2, Pallas kernels: 143 us -> 122 us  [exchange_and_reduce(): pl.pallas_call(functools.partial(reduce_kernel, firsts, rows is not None)...]
    ppermute x2 -> x1, starting transfers between devices: 15.2 us -> 3.21 us  [from_partner(): return lax.ppermute(value, 'tensor', [(0, 1), (1, 0)])]
    unnamed x100 -> x92, local copies, waits for them, and re-layouts: 7.67 us -> 7.86 us
  transfers between devices with their start and end apart: 2 -> 1, of which waited for: 2 -> 1; matrix products, arithmetic and copies ran while one was open for 0% -> 0% of each run, Pallas kernels for 0% -> 0%
where the time goes in v2:
time: 306 us; the launch traced here: 305 us
  Pallas kernels  179 us (58%)
  waiting for transfers between devices  45.6 us (15%)
  matrix products  43.2 us (14%)
  local copies, waits for them, and re-layouts  16.7 us (5%)
  other arithmetic  16.3 us (5%)
  starting transfers between devices  3.21 us (1%)
    pallas_call x2, Pallas kernels, exchange_and_reduce(): pl.pallas_call(functools.partial(reduce_kernel, firsts, rows is not None)...  122 us
    pallas_call x1, Pallas kernels, attend_backward(): pl.pallas_call(attend_back_kernel, out_shape=[jax.ShapeDtypeStruct(terms....  49.5 us
    ppermute x1, waiting for transfers between devices, from_partner(): return lax.ppermute(value, 'tensor', [(0, 1), (1, 0)])  45.6 us
    dot_general x6, matrix products, contract_rows(): jnp.einsum('ta,tb->ab', left, right, preferred_element_type=jnp.float32)  20.5 us
    dot_general x6, matrix products, contract_cols(): jnp.einsum('ta,ba->tb', left, right, preferred_element_type=jnp.float32)  13.2 us
    dot_general x6, matrix products, fdot(): return jnp.dot(left, right, preferred_element_type=jnp.float32)  9.6 us
    unnamed x92, local copies, waits for them, and re-layouts  7.86 us
    pallas_call x1, Pallas kernels, attend_forward(): pl.pallas_call(attend_kernel, out_shape=[jax.ShapeDtypeStruct(query.shape...  7.55 us
  transfers between devices with their start and end apart: 1, of which 1 were waited for; matrix products, arithmetic and copies ran while one was open for 0% of the time, Pallas kernels for 0%

profile of v2, /device:TPU:0, one launch (start us, length us, event | category | flops | bytes accessed | tf_op | source)
XLA Modules:
  0.0 305.2 jit_solution(2218642219504715158)
XLA Ops:
  4.2 2.1 convolution_convert_fusion.1.k_ref
  8.5 7.5 %shard_map.305 = (bf16[512,512]{1,0:T(8,128)(2,1)S(1)}, f32[8,512]{1,0:T(8,128)S(1)}) custom-call(bf16[512,512]{1,0:T(8,128)(2,1)S(1)} %fusion.23.q_ref, bf16[512,512]{1,0:T(8,128)(2,1)S(1)} %convolution_convert_fusion.1.k_ref, bf16[512,512]{1,0:T(8,128)(2,1)S(1)} %fusion.22.v_ref, s32[512,1]{1,0:T(8,128)S(1)} %copy.35.column_ref, s32[1,512]{1,0:T(1,128)S(1)} %bitcast.62), custom_call_target="tpu_custom_call" | custom-call | tf_op jit(solution)/shard_map/pallas_call | solution.py:401
  16.8 3.2 %collective-permute-start = (f32[512,1024]{1,0:T(8,128)S(1)}, f32[512,1024]{1,0:T(8,128)S(1)}, u32[]{:S(2)}, u32[]{:S(2)}) collective-permute-start(f32[512,1024]{1,0:T(8,128)S(1)} %fusion.51), channel_id=1, source_target_pairs={{0,1},{1,0},{2,3},{3,2},{4,5},{5,4},{6,7},{7,6},{8,9},{9,8},{10,11... | collective-permute-start | bytes 6291464 | tf_op jit(solution)/shard_map/ppermute | solution.py:311
  20.0 45.6 %collective-permute-done = f32[512,1024]{1,0:T(8,128)S(1)} collective-permute-done((f32[512,1024]{1,0:T(8,128)S(1)}, f32[512,1024]{1,0:T(8,128)S(1)}, u32[]{:S(2)}, u32[]{:S(2)}) %collective-permute-start) | collective-permute-done | bytes 2097184 | tf_op jit(solution)/shard_map/ppermute | solution.py:311
  66.5 2.1 copy-done.37
  68.6 2.5 fusion.34
  71.2 2.8 fusion.35.terms_ref
  74.0 5.0 %fusion.50 = (f32[2048]{0:T(1024)S(1)}, bf16[512,2048]{1,0:T(8,128)(2,1)S(1)}) fusion(f32[512,2048]{1,0:T(8,128)S(1)} %fusion.34, f32[2048]{0:T(1024)S(1)} %copy-done.38, bf16[2048,1024]{1,0:T(8,128)(2,1)S(1)} %copy-done.36, f32[512,1024]{1,0:T(8,128)S(1)} %copy-done.21), kind=kOutput, calls=%fused_computation.80 | convolution fusion | flops 2170025984 | bytes 12599296 | tf_op jit(solution)/shard_map/ta,ba->tb/dot_general | solution.py:348
  79.0 5.8 %fusion.31 = f32[2048,1024]{0,1:T(8,128)} fusion(f32[512,1024]{1,0:T(8,128)S(1)} %copy-done.21, f32[512,2048]{1,0:T(8,128)S(1)} %fusion.34, f32[2048]{0:T(1024)S(1)} %copy-done.38), kind=kOutput, calls=%fused_computation.51 | convolution fusion | flops 2158493696 | bytes 14688256 | tf_op jit(solution)/shard_map/ta,tb->ab/dot_general | solution.py:344
  84.8 3.7 %fusion.26.refs_0_ = f32[512,1024]{1,0:T(8,128)} fusion(bf16[1024,2048]{1,0:T(8,128)(2,1)S(1)} %copy-done.37, bf16[512,2048]{1,0:T(8,128)(2,1)S(1)} %get-tuple-element.76), kind=kOutput, calls=%fused_computation.46 | convolution fusion | flops 2147483648 | bytes 8388608 | tf_op jit(solution)/shard_map/ta,ba->tb/dot_general | solution.py:348
  88.5 5.9 %fusion.24 = f32[1024,2048]{1,0:T(8,128)} fusion(bf16[512,2048]{1,0:T(8,128)(2,1)S(1)} %get-tuple-element.76, f32[512,1024]{1,0:T(8,128)S(1)} %get-tuple-element.64, f32[1024]{0:T(1024)S(1)} %copy-done.39, f32[1024]{0:T(1024)S(1)} %copy-done.32, f32[512]{0:T(512)S(1)} %add_rsqrt_fusion, f32[512]{0:T(512)S(1)} %broadcast_multiply_fusion.4), kind=kOutput, calls=%fused_computation.44 | convolution fusion | flops 2150105088 | bytes 12595200 | tf_op jit(solution)/shard_map/ta,tb->ab/dot_general | solution.py:344
  94.3 66.0 %shard_map.306 = (f32[512,1024]{1,0:T(8,128)}, f32[16,2048]{1,0:T(8,128)}, f32[16,2048]{1,0:T(8,128)}) custom-call(f32[512,1024]{1,0:T(8,128)} %fusion.26.refs_0_, f32[4,2,4,2,16,2048]{5,4,3,2,1,0:T(8,128)} %bitcast.67, f32[4,2,4,2,16,2048]{5,4,3,2,1,0:T(8,128)} %bitcast.68), custom_call_target="tpu_custom_call" | custom-call | tf_op jit(solution)/shard_map/pallas_call | solution.py:298
  160.4 4.0 %multiply_reduce_fusion = (f32[1024]{0:T(1024)S(1)}, f32[512]{0:T(512)S(1)}, f32[512]{0:T(512)S(1)}, f32[1024]{0:T(1024)S(1)}, f32[512,1024]{1,0:T(8,128)S(1)}) fusion(f32[512,1024]{1,0:T(8,128)} %copy-done.10, f32[512]{0:T(512)S(1)} %add_rsqrt_fusion, f32[512]{0:T(512)S(1)} %broadcast_multiply_fusion.4, f32[1024]{0:T(1024)S(1)} %copy-done.32, ...), kind=kLoop, calls=%fused_computation.28 | loop fusion | flops 5239808 | bytes 8409088 | tf_op jit(solution)/shard_map/reduce_sum | solution.py:522
  166.4 2.1 fusion.28
  168.5 49.5 %shard_map.307 = (f32[512,1024]{1,0:T(8,128)S(1)}, bf16[512,512]{1,0:T(8,128)(2,1)S(1)}, bf16[512,512]{1,0:T(8,128)(2,1)S(1)}, bf16[512,512]{1,0:T(8,128)(2,1)S(...) custom-call(f32[512,1024]{1,0:T(8,128)S(1)} %fusion.35.terms_ref, bf16[512,512]{1,0:T(8,128)(2,1)S(1)} %copy-done.8, ...), custom_call_target="tpu_custom_call" | custom-call | tf_op jit(solution)/shard_map/pallas_call | solution.py:462
  218.1 2.2 fusion.40
  221.1 2.3 fusion.38
  224.1 2.2 fusion.36
  226.3 2.3 fusion.46
  228.6 4.8 %concatenate.3.refs_5_ = f32[72,128]{1,0:T(8,128)} concatenate(f32[8,128]{1,0:T(8,128)S(1)} %bitcast.79, f32[8,128]{1,0:T(8,128)S(1)} %bitcast.78, f32[4,128]{1,0:T(4,128)S(1)} %bitcast.64, f32[4,128]{1,0:T(4,128)S(1)} %bitcast.65, f32[8,128]{1,0:T(8,128)S(1)} %bitcast.76, f32[8,128]{1,0:T(8,128)S(1)} %bitcast.74, f32[8,128]{1,0:T(8,128)S(1)} %bitcast.75, ...), dimensions={0} | concatenate | bytes 73728 | tf_op jit(solution)/shard_map/concatenate | solution.py:553
  233.3 55.9 %shard_map.308 = (f32[512,1024]{1,0:T(8,128)}, f32[16,512]{1,0:T(8,128)}, f32[16,512]{1,0:T(8,128)}, f32[16,512]{1,0:T(8,128)}, f32[16,512]{1,0:T(8,128)}, /*index=5*/f32[72,128]{1,0:T(8,128)}) custom-call(f32[512,1024]{1,0:T(8,128)} %get-tuple-element.74.refs_0_, f32[4,2,4,2,16,512]{5,4,3,2,1,0:T(8,128)} %bitcast.69, f32[4,2,4,2,16,512]{5,4,3,2,1,0:T(8,128)} %bitcast.70, ...), custom_call_target="tpu_custom_call" | custom-call | tf_op jit(solution)/shard_map/pallas_call | solution.py:298
  293.2 3.4 %fusion.45 = (f32[512]{0:T(512)S(1)}, f32[512]{0:T(512)S(1)}, f32[512,1024]{1,0:T(8,128)S(1)}) fusion(f32[512]{0:T(512)S(1)} %add_rsqrt_fusion.1, f32[512]{0:T(512)S(1)} %broadcast_multiply_fusion.5, bf16[512,1024]{1,0:T(8,128)(2,1)} %param.18, f32[1024]{0:T(1024)S(1)} %copy-done.34, f32[512,1024]{1,0:T(8,128)} %get-tuple-element.74.refs_0_, ...), kind=kLoop, calls=%fused_computation.76 | loop fusion | flops 4193280 | bytes 7352320 | tf_op jit(solution)/shard_map/reduce_sum | solution.py:325
  297.0 2.0 add_add_fusion.1
  299.5 1.9 fusion.18
  (113 shorter events, 19.2 us)
Async XLA Ops:
  0.7 5.6 %copy-start = (bf16[1024,512]{1,0:T(8,128)(2,1)S(1)}, bf16[1024,512]{1,0:T(8,128)(2,1)}, u32[]{:S(2)}) copy-start(bf16[1024,512]{1,0:T(8,128)(2,1)} %param.24) | copy-start | bytes 3145732
  0.7 3.4 %copy-start.13 = (bf16[512,1024]{1,0:T(8,128)(2,1)S(1)}, bf16[512,1024]{1,0:T(8,128)(2,1)}, u32[]{:S(2)}) copy-start(bf16[512,1024]{1,0:T(8,128)(2,1)} %param.18) | copy-start | bytes 3145732
  0.7 3.3 %copy-start.9 = (s32[512]{0:T(512)S(1)}, s32[512]{0:T(512)}, u32[]{:S(2)}) copy-start(s32[512]{0:T(512)} %param.19) | copy-start | bytes 6148
  0.7 3.4 %copy-start.34 = (f32[1024]{0:T(1024)S(1)}, f32[1024]{0:T(1024)}, u32[]{:S(2)}) copy-start(f32[1024]{0:T(1024)} %param.20) | copy-start | bytes 12292
  0.7 3.4 %copy-start.40 = (f32[1024]{0:T(1024)S(1)}, f32[1024]{0:T(1024)}, u32[]{:S(2)}) copy-start(f32[1024]{0:T(1024)} %param.21) | copy-start | bytes 12292
  8.5 8.3 %copy-start.7 = (bf16[512,512]{1,0:T(8,128)(2,1)}, bf16[512,512]{1,0:T(8,128)(2,1)S(1)}, u32[]{:S(2)}) copy-start(bf16[512,512]{1,0:T(8,128)(2,1)S(1)} %fusion.23.q_ref) | copy-start | bytes 1572868
  8.5 7.6 %copy-start.19 = (bf16[512,1024]{1,0:T(8,128)(2,1)S(1)}, bf16[512,1024]{1,0:T(8,128)(2,1)}, u32[]{:S(2)}) copy-start(bf16[512,1024]{1,0:T(8,128)(2,1)} %param.27) | copy-start | bytes 3145732
  16.1 49.6 %copy-start.33 = (f32[1024]{0:T(1024)S(1)}, f32[1024]{0:T(1024)}, u32[]{:S(2)}) copy-start(f32[1024]{0:T(1024)} %param.28) | copy-start | bytes 12292
  16.8 48.8 %collective-permute-start = (f32[512,1024]{1,0:T(8,128)S(1)}, f32[512,1024]{1,0:T(8,128)S(1)}, u32[]{:S(2)}, u32[]{:S(2)}) collective-permute-start(f32[512,1024]{1,0:T(8,128)S(1)} %fusion.51), channel_id=1, source_target_pairs={{0,1},{1,0},{2,3},{3,2},{4,5},{5,4},{6,7},{7,6},{8,9},{9,8},{10,11... | collective-permute-start | bytes 6291464 | tf_op jit(solution)/shard_map/ppermute | solution.py:311
  65.7 2.9 copy-start.37
  66.1 22.3 %copy-start.10 = (f32[512,1024]{1,0:T(8,128)}, f32[512,1024]{1,0:T(8,128)S(1)}, u32[]{:S(2)}) copy-start(f32[512,1024]{1,0:T(8,128)S(1)} %get-tuple-element.64) | copy-start | bytes 6291460
  71.1 2.8 copy-start.21
  160.3 4.0 %copy-start.11 = (f32[512,1024]{1,0:T(8,128)S(1)}, f32[512,1024]{1,0:T(8,128)}, u32[]{:S(2)}) copy-start(f32[512,1024]{1,0:T(8,128)} %copy-done.10) | copy-start | bytes 6291460
  160.3 4.1 %copy-start.22 = (f32[512,1024]{1,0:T(8,128)S(1)}, f32[512,1024]{1,0:T(8,128)}, u32[]{:S(2)}) copy-start(f32[512,1024]{1,0:T(8,128)} %param.35) | copy-start | bytes 6291460
  165.3 3.2 %copy-start.17 = (f32[512,1024]{1,0:T(8,128)}, f32[512,1024]{1,0:T(8,128)S(1)}, u32[]{:S(2)}) copy-start(f32[512,1024]{1,0:T(8,128)S(1)} %get-tuple-element.61) | copy-start | bytes 6291460
  168.5 49.6 %copy-start.15 = (bf16[512,1024]{1,0:T(8,128)(2,1)S(1)}, bf16[512,1024]{1,0:T(8,128)(2,1)}, u32[]{:S(2)}) copy-start(bf16[512,1024]{1,0:T(8,128)(2,1)} %param.18) | copy-start | bytes 3145732
  293.2 3.5 %copy-start.2 = (f32[512,1024]{1,0:T(8,128)S(1)}, f32[512,1024]{1,0:T(8,128)}, u32[]{:S(2)}) copy-start(f32[512,1024]{1,0:T(8,128)} %copy-done.1) | copy-start | bytes 6291460
  293.2 3.8 %copy-start.12 = (f32[512,1024]{1,0:T(8,128)S(1)}, f32[512,1024]{1,0:T(8,128)}, u32[]{:S(2)}) copy-start(f32[512,1024]{1,0:T(8,128)} %copy-done.10) | copy-start | bytes 6291460
  293.2 3.8 %copy-start.35 = (f32[1024]{0:T(1024)S(1)}, f32[1024]{0:T(1024)}, u32[]{:S(2)}) copy-start(f32[1024]{0:T(1024)} %param.34) | copy-start | bytes 12292
  299.4 2.6 copy-start.30
  299.4 3.2 %copy-start.29 = (f32[16,512]{1,0:T(8,128)S(1)}, f32[16,512]{1,0:T(8,128)}, u32[]{:S(2)}) copy-start(f32[16,512]{1,0:T(8,128)} %get-tuple-element.104) | copy-start | bytes 98308
  299.5 3.8 %copy-start.28 = (f32[16,512]{1,0:T(8,128)S(1)}, f32[16,512]{1,0:T(8,128)}, u32[]{:S(2)}) copy-start(f32[16,512]{1,0:T(8,128)} %get-tuple-element.48) | copy-start | bytes 98308
  299.5 4.4 %copy-start.27 = (f32[16,2048]{1,0:T(8,128)S(1)}, f32[16,2048]{1,0:T(8,128)}, u32[]{:S(2)}) copy-start(f32[16,2048]{1,0:T(8,128)} %get-tuple-element.111) | copy-start | bytes 393220
  299.5 5.1 %copy-start.26 = (f32[16,2048]{1,0:T(8,128)S(1)}, f32[16,2048]{1,0:T(8,128)}, u32[]{:S(2)}) copy-start(f32[16,2048]{1,0:T(8,128)} %get-tuple-element.50) | copy-start | bytes 393220
  (20 other events, 40.8 us)
